TPU v7x, 512 devices: a whole 4x8x8 slice. The times are simulated.
512 devices in a mesh: dp: 16 (over z_hi, x), expert: 32 (over z_lo, y, core).
Axes of the slice: x: 4, y: 8, z: 8 (z_hi: 4, z_lo: 2; z = z_hi * 2 + z_lo), core: 2. Of those that a mesh axis runs over, the one named last changes fastest.
Arguments:
- tokens: bfloat16 [6144, 6144], P('expert', 'dp'), may hold values from -6 to 6
- expert_of: int32 [6144], P('expert'), may hold values from 0 to 31, as said below
- router_weight: float32 [6144], P('expert'), may hold values from 0.2 to 1
- cotangent: bfloat16 [6144, 6144], P('expert', 'dp'), may hold values from -6 to 6
- gate_up_weight: bfloat16 [32, 2, 6144, 1024], P('expert', None, 'dp'), may hold values from -0.078125 to 0.078125
- down_weight: bfloat16 [32, 1024, 6144], P('expert', None, 'dp'), may hold values from -0.1875 to 0.1875
Outputs:
- layer_out: bfloat16 [6144, 6144], P('expert', 'dp')
- grad_tokens: bfloat16 [6144, 6144], P('expert', 'dp')
- grad_gate_up: bfloat16 [32, 2, 6144, 1024], P('expert', None, 'dp')
- grad_down: bfloat16 [32, 1024, 6144], P('expert', None, 'dp')
Inputs may be any that keep to these rules, and one draw needn't show every extreme that they name: `expert_of`: take the tokens in aligned blocks of 192, one block for each index of expert. One expert, the same for all blocks, is named by exactly 12 tokens of every block; every other expert is named by at most 9 tokens of a block, and in every block some other expert by exactly 9.
All inputs are finite; a program needn't handle non-finite values.
Results may differ from a plain program's by a relative error of at most 0.0058.
Values may be sent and summed in bfloat16 or wider, within the bound.
No kernel may reach another device: no remote copies, remote signals or barrier semaphores. Data moves between devices by JAX's collectives and lax.ppermute only.
A program may use at most 64 MiB of HBM per device.

v0:
```python
import jax
import jax.numpy as jnp
from jax import lax
from jax.sharding import PartitionSpec as P


def slot_dispatch(base_index, kept, width):
    position = jnp.sum((jnp.cumsum(kept, axis=0) - kept) * kept, axis=1)
    is_live = jnp.sum(kept, axis=1) > 0
    slot_index = jnp.where(is_live, base_index + position, -1)
    return (slot_index[None, :] == jnp.arange(width, dtype=jnp.int32)[:, None]).astype(jnp.bfloat16)


def expert_pass(row_block, fetch_cotangent, gate_up_slab, down_slab):
    partial_value = jnp.einsum(
        "rd,kdf->kfr", row_block, gate_up_slab, preferred_element_type=jnp.float32
    )
    shares = lax.psum_scatter(partial_value, "dp", scatter_dimension=1, tiled=True)
    gate_value = shares[0]
    up_value = shares[1]
    sigmoid_gate = jax.nn.sigmoid(gate_value)
    activated = gate_value * sigmoid_gate
    hidden = (activated * up_value).astype(jnp.bfloat16)
    cot_rows = fetch_cotangent()
    segment = lax.all_gather(hidden, "dp", axis=0, tiled=True)
    out_acc = lax.dot_general(
        segment, down_slab, (((0,), (0,)), ((), ())), preferred_element_type=jnp.float32
    )
    grad_rows = jnp.dot(segment, cot_rows, preferred_element_type=jnp.float32)
    down_grad = grad_rows
    out_acc, down_grad = (out_acc, down_grad)
    expert_out = out_acc.astype(jnp.bfloat16)
    grad_partial = lax.dot_general(
        down_slab, cot_rows, (((1,), (1,)), ((), ())), preferred_element_type=jnp.float32
    )
    hidden_grad = lax.psum_scatter(grad_partial, "dp", scatter_dimension=0, tiled=True)
    gate_grad = hidden_grad * up_value * sigmoid_gate * (1.0 + gate_value * (1.0 - sigmoid_gate))
    up_grad = hidden_grad * activated
    gate_up_grad = jnp.stack([gate_grad, up_grad], axis=0).astype(jnp.bfloat16)
    segment = lax.all_gather(gate_up_grad, "dp", axis=1, tiled=True)
    row_grad = jnp.einsum("kfr,kdf->rd", segment, gate_up_slab, preferred_element_type=jnp.float32)
    grad_cols = jnp.einsum("rd,kfr->kdf", row_block, segment, preferred_element_type=jnp.float32)
    weight_grad = grad_cols
    row_grad, weight_grad = (row_grad, weight_grad)
    return (expert_out, row_grad.astype(jnp.bfloat16), weight_grad, down_grad)


def routed_pass(dispatch, tokens, scaled, gate_up_slab, down_slab):
    send_tokens = jnp.dot(dispatch, tokens, preferred_element_type=jnp.float32).astype(jnp.bfloat16)
    send_cotangent = jnp.dot(dispatch, scaled, preferred_element_type=jnp.float32).astype(
        jnp.bfloat16
    )
    recv_tokens, recv_cotangent = (
        lax.all_to_all(send_tokens, "expert", split_axis=0, concat_axis=0, tiled=True),
        lax.all_to_all(send_cotangent, "expert", split_axis=0, concat_axis=0, tiled=True),
    )

    def fetch_cotangent():
        return recv_cotangent

    expert_out, row_grad, weight_grad, down_grad = expert_pass(
        recv_tokens, fetch_cotangent, gate_up_slab, down_slab
    )
    back_out, back_grad = (
        lax.all_to_all(expert_out, "expert", split_axis=0, concat_axis=0, tiled=True),
        lax.all_to_all(row_grad, "expert", split_axis=0, concat_axis=0, tiled=True),
    )
    out_tok = lax.dot_general(
        dispatch, back_out, (((0,), (0,)), ((), ())), preferred_element_type=jnp.float32
    )
    grad_tok = lax.dot_general(
        dispatch, back_grad, (((0,), (0,)), ((), ())), preferred_element_type=jnp.float32
    )
    return (out_tok, grad_tok, weight_grad, down_grad)


def shards(tokens, expert_of, router_weight, cotangent, gate_up_weight, down_weight):
    expert_total = lax.axis_size("expert")
    token_count = tokens.shape[0]
    gate_up_slab = gate_up_weight[0]
    down_slab = down_weight[0]
    scaled = (router_weight[:, None] * cotangent.astype(jnp.float32)).astype(jnp.bfloat16)
    expert_ids = jnp.arange(expert_total, dtype=jnp.int32)
    onehot = (expert_of[:, None] == expert_ids[None, :]).astype(jnp.int32)
    hot_room = 2 * token_count // expert_total
    dispatch = slot_dispatch(expert_of * hot_room, onehot, expert_total * hot_room)
    out_tok, grad_tok, weight_grad, down_grad = routed_pass(
        dispatch, tokens, scaled, gate_up_slab, down_slab
    )
    layer_out = (router_weight[:, None] * out_tok).astype(jnp.bfloat16)
    grad_tokens = grad_tok.astype(jnp.bfloat16)
    return (
        layer_out,
        grad_tokens,
        weight_grad.astype(jnp.bfloat16)[None],
        down_grad.astype(jnp.bfloat16)[None],
    )


def solution(mesh):
    placed = (
        P("expert", "dp"),
        P("expert"),
        P("expert"),
        P("expert", "dp"),
        P("expert", None, "dp", None),
        P("expert", None, "dp"),
    )
    return jax.shard_map(
        shards,
        mesh=mesh,
        in_specs=placed,
        out_specs=(
            P("expert", "dp"),
            P("expert", "dp"),
            P("expert", None, "dp", None),
            P("expert", None, "dp"),
        ),
        check_vma=False,
    )
```

profile of v0, /device:TPU:1, one launch (start us, length us, event | category | flops | bytes accessed | tf_op | source)
XLA Modules:
  0.0 450.4 jit_solution(14273278014618224155)
XLA Ops:
  7.2 0.8 iota_compare_fusion.5
  8.9 0.7 fusion.33
  9.7 0.7 compare_select_fusion
  10.3 1.2 convolution_convert_fusion.4
  11.6 24.5 %all_to_all.48 = bf16[32,12,384]{2,1,0:T(8,128)(2,1)S(1)} all-to-all(bf16[32,12,384]{2,1,0:T(8,128)(2,1)S(1)} %all_to_all.32), channel_id=1, replica_groups=mesh['dp'=16,'expert'=32] {'expert'}, dimensions={0} | all-to-all | bytes 589824 | tf_op jit(solution)/shard_map/all_to_all | solution.py:54
  36.2 2.7 convolution_bitcast_fusion
  38.8 5.8 %copy.20 = f32[2,1024,384]{2,0,1:T(2,128)} copy(f32[2,1024,384]{1,2,0:T(8,128)} %convolution_bitcast_fusion) | data formatting | bytes 6291456 | tf_op jit(solution)/shard_map/rd,kdf->kfr/dot_general | solution.py:15
  44.8 0.8 copy-done.3
  46.0 18.9 %all_to_all.49 = bf16[32,12,384]{2,1,0:T(8,128)(2,1)S(1)} all-to-all(bf16[32,12,384]{2,1,0:T(8,128)(2,1)S(1)} %all_to_all.38), channel_id=1, replica_groups=mesh['dp'=16,'expert'=32] {'expert'}, dimensions={0} | all-to-all | bytes 589824 | tf_op jit(solution)/shard_map/all_to_all | solution.py:55
  65.0 1.7 convolution_bitcast_fusion.1
  66.7 1.6 copy.28
  68.4 1.3 dynamic-slice
  70.4 169.5 %all-reduce.4.cloned.1.call-done = f32[2,1024,384]{2,0,1:T(2,128)} async-done(((f32[2,1024,384]{2,0,1:T(2,128)}), f32[2,1024,384]{2,0,1:T(2,128)}) %all-reduce.4.cloned.1.call-update) | async-done | bytes 3145744
  239.9 1.2 constant_dynamic-slice_fusion
  241.1 96.5 %reduce-scatter.4.cloned.1.call-done = f32[64,384]{1,0:T(8,128)} async-done(((f32[1024,384]{1,0:T(8,128)}), f32[64,384]{1,0:T(8,128)}) %reduce-scatter.4.cloned.1.call-update) | async-done | bytes 98320 | tf_op jit(solution)/shard_map/reduce_scatter | solution.py:36
  337.7 0.9 fusion.31
  338.6 0.7 copy.24
  339.4 43.4 %all_gather.6 = bf16[1024,384]{1,0:T(8,128)(2,1)S(1)} all-gather(bf16[64,384]{1,0:T(8,128)(2,1)S(1)} %get-tuple-element.22), channel_id=1, replica_groups=mesh['dp'=16,'expert'=32] {'dp'}, dimensions={0}, use_global_device_ids=true | all-gather | bytes 835584 | tf_op jit(solution)/shard_map/all_gather | solution.py:25
  382.8 1.3 convolution_convert_fusion.3
  384.2 1.8 all_to_all.35
  385.9 21.3 %all-to-all-start.1 = ((bf16[32,12,384]{2,1,0:T(8,128)(2,1)}), bf16[32,12,384]{2,1,0:T(8,128)(2,1)S(1)}, u32[]{:S(2)}, u32[]{:S(2)}) async-start(bf16[32,12,384]{2,1,0:T(8,128)(2,1)} %all_to_all.35), calls=%async_computation.1 | async-start | bytes 786432 | tf_op jit(solution)/shard_map/all_to_all | solution.py:65
  407.3 2.4 fusion.12
  409.7 0.9 all_to_all.41
  410.6 10.8 %all-to-all-done.1 = bf16[32,12,384]{2,1,0:T(8,128)(2,1)S(1)} async-done(((bf16[32,12,384]{2,1,0:T(8,128)(2,1)}), bf16[32,12,384]{2,1,0:T(8,128)(2,1)S(1)}, u32[]{:S(2)}, u32[]{:S(2)}) %all-to-all-start.1) | async-done | bytes 294944 | tf_op jit(solution)/shard_map/all_to_all | solution.py:65
  421.3 6.2 %all-to-all-start.3 = ((bf16[32,12,384]{2,1,0:T(8,128)(2,1)}), bf16[32,12,384]{2,1,0:T(8,128)(2,1)}, u32[]{:S(2)}, u32[]{:S(2)}) async-start(bf16[32,12,384]{2,1,0:T(8,128)(2,1)} %all_to_all.41), calls=%async_computation.3 | async-start | bytes 786432 | tf_op jit(solution)/shard_map/all_to_all | solution.py:66
  427.5 1.5 fusion.6
  429.1 1.0 fusion.17
  430.1 2.5 fusion.3
  432.7 1.6 copy.27
  434.3 7.5 %all-to-all-done.3 = bf16[32,12,384]{2,1,0:T(8,128)(2,1)} async-done(((bf16[32,12,384]{2,1,0:T(8,128)(2,1)}), bf16[32,12,384]{2,1,0:T(8,128)(2,1)}, u32[]{:S(2)}, u32[]{:S(2)}) %all-to-all-start.3) | async-done | bytes 294944 | tf_op jit(solution)/shard_map/all_to_all | solution.py:66
  441.8 1.1 all_to_all.43
  442.9 1.0 convolution_convert_fusion.5
  (29 shorter events, 1.8 us)
Async XLA Ops:
  7.2 29.0 %copy-start = (bf16[1,2,384,1024]{3,2,1,0:T(8,128)(2,1)S(1)}, bf16[1,2,384,1024]{3,2,1,0:T(8,128)(2,1)}, u32[]{:S(2)}) copy-start(bf16[1,2,384,1024]{3,2,1,0:T(8,128)(2,1)} %param.10) | copy-start | bytes 4718596
  7.2 232.8 %all-reduce.4.cloned.1.call-start = ((), (), s32[]{:S(2)}) async-start(), calls=%async_computation.7 | async-start | bytes 6291456
  36.1 2.7 copy-start.1
  44.7 0.9 copy-start.3
  44.7 0.9 copy-start.4
  44.7 293.0 %reduce-scatter.4.cloned.1.call-start = ((), (), s32[]{:S(2)}) async-start(), calls=%async_computation.6 | async-start | bytes 1671168 | tf_op jit(solution)/shard_map/reduce_scatter | solution.py:36
  68.3 314.5 %copy-start.2 = (bf16[1,1024,384]{2,1,0:T(8,128)(2,1)S(1)}, bf16[1,1024,384]{2,1,0:T(8,128)(2,1)}, u32[]{:S(2)}) copy-start(bf16[1,1024,384]{2,1,0:T(8,128)(2,1)} %param.11) | copy-start | bytes 2359300
  68.4 338.9 %all-gather.2.cloned.1.call-start = ((), (), s32[]{:S(2)}) async-start(), calls=%async_computation.5 | async-start | bytes 1671168 | tf_op jit(solution)/shard_map/all_gather | solution.py:40
  385.9 35.4 %all-to-all-start.1 = ((bf16[32,12,384]{2,1,0:T(8,128)(2,1)}), bf16[32,12,384]{2,1,0:T(8,128)(2,1)S(1)}, u32[]{:S(2)}, u32[]{:S(2)}) async-start(bf16[32,12,384]{2,1,0:T(8,128)(2,1)} %all_to_all.35), calls=%async_computation.1 | async-start | bytes 786432 | tf_op jit(solution)/shard_map/all_to_all | solution.py:65
  421.3 20.5 %all-to-all-start.3 = ((bf16[32,12,384]{2,1,0:T(8,128)(2,1)}), bf16[32,12,384]{2,1,0:T(8,128)(2,1)}, u32[]{:S(2)}, u32[]{:S(2)}) async-start(bf16[32,12,384]{2,1,0:T(8,128)(2,1)} %all_to_all.41), calls=%async_computation.3 | async-start | bytes 786432 | tf_op jit(solution)/shard_map/all_to_all | solution.py:66
Sparse Core Ops, SparseCore 0:
  44.8 195.0 all-reduce.3
  244.6 93.0 reduce-scatter.3
  341.3 60.7 all-gather.1
where the time goes:
time: 451 us; the launch traced here: 450 us
  waiting for transfers between devices  284 us (63%)
  blocking collectives  86.8 us (19%)
  starting transfers between devices  27.6 us (6%)
  local copies, waits for them, and re-layouts  17.4 us (4%)
  matrix products  15.7 us (3%)
  between operations  14.5 us (3%)
    unnamed x4, waiting for transfers between devices  170 us
    reduce_scatter x1, waiting for transfers between devices, expert_pass(): lax.psum_scatter(grad_partial, 'dp', scatter_dimension=0, tiled=True)  96.5 us
    all_gather x1, blocking collectives, expert_pass(): segment = lax.all_gather(hidden, 'dp', axis=0, tiled=True)  43.4 us
    all_to_all x1, blocking collectives, routed_pass(): lax.all_to_all(send_tokens, 'expert', split_axis=0, concat_axis=0, tiled=...  24.5 us
    all_to_all x1, starting transfers between devices, routed_pass(): lax.all_to_all(expert_out, 'expert', split_axis=0, concat_axis=0, tiled=T...  21.3 us
    all_to_all x1, blocking collectives, routed_pass(): lax.all_to_all(send_cotangent, 'expert', split_axis=0, concat_axis=0, til...  18.9 us
    all_to_all x1, waiting for transfers between devices, routed_pass(): lax.all_to_all(expert_out, 'expert', split_axis=0, concat_axis=0, tiled=T...  10.8 us
  transfers between devices with their start and end apart: 5, of which 4 were waited for; matrix products, arithmetic and copies ran while one was open for 4% of the time, Pallas kernels for 0%

commit v1 on v0

v1 whole, which is shorter than its diff:
```python
import jax
import jax.numpy as jnp
from jax import lax
from jax.sharding import Mesh, PartitionSpec as P

NX = 4
NZ = 4
TOKEN_AXES = ("zl", "y", "core")


def slots_of(expert_of, width, room):
    count = expert_of.shape[0]
    index = jnp.arange(count, dtype=jnp.int32)
    earlier = (expert_of[:, None] == expert_of[None, :]) & (index[None, :] < index[:, None])
    position = jnp.sum(earlier.astype(jnp.int32), axis=1)
    slot = expert_of * room + position
    return (slot[None, :] == jnp.arange(width, dtype=jnp.int32)[:, None]).astype(jnp.bfloat16)


def dot(a, b, dims):
    return lax.dot_general(a, b, (dims, ((), ())), preferred_element_type=jnp.float32)


def sum_blocks(blocks):
    b = [blocks[i].astype(jnp.float32) for i in range(blocks.shape[0])]
    return (b[0] + b[1]) + (b[2] + b[3])


def scatter_sum(partial):
    rows, width = partial.shape
    first = lax.all_to_all(partial.reshape(NX, rows // NX, width), "x", 0, 0, tiled=True)
    first = sum_blocks(first).astype(jnp.bfloat16)
    second = lax.all_to_all(first.reshape(NZ, rows // NX // NZ, width), "zh", 0, 0, tiled=True)
    return sum_blocks(second)


def gather_rows(part):
    return lax.all_gather(lax.all_gather(part, "zh", axis=0, tiled=True), "x", axis=0, tiled=True)


def shards(tokens, expert_of, router_weight, cotangent, gate_up_weight, down_weight):
    tok, feat = tokens.shape
    experts = 32
    room = 2 * tok // experts
    rows = experts * room
    w_gate = gate_up_weight[0, 0]
    w_up = gate_up_weight[0, 1]
    w_down = down_weight[0]
    ff = w_gate.shape[1]
    scaled = (router_weight[:, None] * cotangent.astype(jnp.float32)).astype(jnp.bfloat16)
    dispatch = slots_of(expert_of, rows, room)
    send = jnp.concatenate(
        [dot(dispatch, tokens, ((1,), (0,))), dot(dispatch, scaled, ((1,), (0,)))], axis=1
    ).astype(jnp.bfloat16)
    recv = lax.all_to_all(
        send.reshape(experts, room, 2 * feat), TOKEN_AXES, 0, 0, tiled=True
    ).reshape(rows, 2 * feat)
    x_rows = recv[:, :feat]
    s_rows = recv[:, feat:]

    partial = jnp.concatenate(
        [
            dot(x_rows, w_gate, ((1,), (0,))).astype(jnp.bfloat16),
            dot(x_rows, w_up, ((1,), (0,))).astype(jnp.bfloat16),
            dot(s_rows, w_down, ((1,), (1,))).astype(jnp.bfloat16),
        ],
        axis=1,
    )
    total = scatter_sum(partial)
    gate = total[:, :ff]
    up = total[:, ff : 2 * ff]
    hidden_grad = total[:, 2 * ff :]
    sig = jax.nn.sigmoid(gate)
    act = gate * sig
    part = jnp.concatenate(
        [
            act * up,
            hidden_grad * up * sig * (1.0 + gate * (1.0 - sig)),
            hidden_grad * act,
        ],
        axis=1,
    ).astype(jnp.bfloat16)
    full = gather_rows(part)
    hidden = full[:, :ff]
    gate_grad = full[:, ff : 2 * ff]
    up_grad = full[:, 2 * ff :]

    expert_out = dot(hidden, w_down, ((1,), (0,)))
    row_grad = dot(gate_grad, w_gate, ((1,), (1,))) + dot(up_grad, w_up, ((1,), (1,)))
    back = jnp.concatenate([expert_out, row_grad], axis=1).astype(jnp.bfloat16)
    back = lax.all_to_all(
        back.reshape(experts, room, 2 * feat), TOKEN_AXES, 0, 0, tiled=True
    ).reshape(rows, 2 * feat)
    grad_gate = dot(x_rows, gate_grad, ((0,), (0,)))
    grad_up = dot(x_rows, up_grad, ((0,), (0,)))
    grad_down = dot(hidden, s_rows, ((0,), (0,)))
    out = dot(dispatch, back, ((0,), (0,)))
    layer_out = (router_weight[:, None] * out[:, :feat]).astype(jnp.bfloat16)
    grad_tokens = out[:, feat:].astype(jnp.bfloat16)
    return (
        layer_out,
        grad_tokens,
        jnp.stack([grad_gate, grad_up]).astype(jnp.bfloat16)[None],
        grad_down.astype(jnp.bfloat16)[None],
    )


def solution(mesh):
    fine = Mesh(mesh.devices.reshape(NZ, NX, 2, 8, 2), ("zh", "x", "zl", "y", "core"))
    dp = ("zh", "x")
    ex = TOKEN_AXES
    return jax.shard_map(
        shards,
        mesh=fine,
        in_specs=(P(ex, dp), P(ex), P(ex), P(ex, dp), P(ex, None, dp, None), P(ex, None, dp)),
        out_specs=(P(ex, dp), P(ex, dp), P(ex, None, dp, None), P(ex, None, dp)),
        check_vma=False,
    )
```

time: 451 us -> 204 us (0.45)
  waiting for transfers between devices: 284 us -> 57.3 us
  starting transfers between devices: 27.6 us -> 8.69 us
  local copies, waits for them, and re-layouts: 17.4 us -> 3.8 us
  blocking collectives: 86.8 us -> 98.1 us
    unnamed x4 -> x1, waiting for transfers between devices: 170 us -> 0.02 us
    reduce_scatter x1 -> x0, waiting for transfers between devices: 96.5 us -> none  [expert_pass(): lax.psum_scatter(grad_partial, 'dp', scatter_dimension=0, tiled=True)]
    all_gather x1, waiting for transfers between devices: 0.02 us -> 43.5 us  [gather_rows(): lax.all_gather(lax.all_gather(part, 'zh', axis=0, tiled=True), 'x', axis=...]
    all_to_all x2 -> x3, blocking collectives: 43.4 us -> 83 us  [the longest x1 31.6 us: shards(): lax.all_to_all(send.reshape(experts, room, 2 * feat), TOKEN_AXES, 0, 0, t...]
    all_gather x1, blocking collectives: 43.4 us -> 15.1 us  [gather_rows(): lax.all_gather(part, 'zh', axis=0, tiled=True)]
    all_to_all x2 -> x1, starting transfers between devices: 27.5 us -> 8.65 us  [shards(): lax.all_to_all(back.reshape(experts, room, 2 * feat), TOKEN_AXES, 0, 0, t...]
    dot_general x1, local copies, waits for them, and re-layouts: 5.85 us -> 0.17 us  [dot(): lax.dot_general(a, b, (dims, ((), ())), preferred_element_type=jnp.float32)]
    unnamed x13 -> x6, local copies, waits for them, and re-layouts: 5.42 us -> 0.02 us
  transfers between devices with their start and end apart: 5 -> 2, of which waited for: 4 -> 2; matrix products, arithmetic and copies ran while one was open for 4% -> 4% of each run, Pallas kernels for 0% -> 0%
where the time goes in v1:
time: 204 us; the launch traced here: 203 us
  blocking collectives  98.1 us (48%)
  waiting for transfers between devices  57.3 us (28%)
  matrix products  16.1 us (8%)
  between operations  14.2 us (7%)
  starting transfers between devices  8.69 us (4%)
  other arithmetic  4.44 us (2%)
  local copies, waits for them, and re-layouts  3.8 us (2%)
    all_gather x1, waiting for transfers between devices, gather_rows(): lax.all_gather(lax.all_gather(part, 'zh', axis=0, tiled=True), 'x', axis=...  43.5 us
    all_to_all x1, blocking collectives, shards(): lax.all_to_all(send.reshape(experts, room, 2 * feat), TOKEN_AXES, 0, 0, t...  31.6 us
    all_to_all x1, blocking collectives, scatter_sum(): lax.all_to_all(partial.reshape(NX, rows // NX, width), 'x', 0, 0, tiled=T...  30.4 us
    all_to_all x1, blocking collectives, scatter_sum(): lax.all_to_all(first.reshape(NZ, rows // NX // NZ, width), 'zh', 0, 0, ti...  21 us
    dot_general x12, matrix products, dot(): lax.dot_general(a, b, (dims, ((), ())), preferred_element_type=jnp.float32)  16.1 us
    all_gather x1, blocking collectives, gather_rows(): lax.all_gather(part, 'zh', axis=0, tiled=True)  15.1 us
    all_to_all x1, waiting for transfers between devices, shards(): lax.all_to_all(back.reshape(experts, room, 2 * feat), TOKEN_AXES, 0, 0, t...  13.8 us
    all_to_all x1, starting transfers between devices, shards(): lax.all_to_all(back.reshape(experts, room, 2 * feat), TOKEN_AXES, 0, 0, t...  8.65 us
  transfers between devices with their start and end apart: 2, of which 2 were waited for; matrix products, arithmetic and copies ran while one was open for 4% of the time, Pallas kernels for 0%

profile of v1, /device:TPU:1, one launch (start us, length us, event | category | flops | bytes accessed | tf_op | source)
XLA Modules:
  0.0 202.6 jit_solution(1716345662355274634)
XLA Ops:
  7.2 0.9 convert_reduce_fusion
  8.2 0.7 multiply_add_fusion
  8.9 1.2 convolution_convert_fusion.7
  10.2 1.2 convolution_convert_fusion.8
  11.5 0.1 pad_maximum_fusion.2
  11.5 31.6 %all_to_all.20 = bf16[32,12,768]{2,1,0:T(8,128)(2,1)S(1)} all-to-all(bf16[32,12,768]{2,1,0:T(8,128)(2,1)S(1)} %pad_maximum_fusion.2), channel_id=1, replica_groups=mesh['zh'=4,'x'=4,'zl'=2,'y'=8,'core'=2] {'zl','y','core'}, dimensions={0} | all-to-all | bytes 1179648 | tf_op jit(solution)/shard_map/all_to_all | solution.py:55
  43.1 0.1 reshape.84
  43.3 1.8 convolution_convert_fusion.4
  45.1 0.6 convolution_convert_fusion.5
  45.7 0.6 convolution_convert_fusion.3
  46.3 0.2 pad_maximum_fusion
  46.5 30.4 %all_to_all.21 = bf16[4,96,3072]{2,1,0:T(8,128)(2,1)S(1)} all-to-all(bf16[4,96,3072]{2,1,0:T(8,128)(2,1)S(1)} %bitcast.28), channel_id=1, replica_groups=mesh['zh'=4,'x'=4,'zl'=2,'y'=8,'core'=2] {'x'}, dimensions={0} | all-to-all | bytes 4718592 | tf_op jit(solution)/shard_map/all_to_all | solution.py:31
  76.9 0.3 add_convert_fusion
  77.2 21.0 %all_to_all.22 = bf16[4,24,3072]{2,1,0:T(8,128)(2,1)S(1)} all-to-all(bf16[4,24,3072]{2,1,0:T(8,128)(2,1)S(1)} %bitcast.29), channel_id=1, replica_groups=mesh['zh'=4,'x'=4,'zl'=2,'y'=8,'core'=2] {'zh'}, dimensions={0} | all-to-all | bytes 1179648 | tf_op jit(solution)/shard_map/all_to_all | solution.py:33
  98.4 15.1 %all_gather.6 = bf16[96,3072]{1,0:T(8,128)(2,1)} all-gather(bf16[24,3072]{1,0:T(8,128)(2,1)S(1)} %pad_maximum_fusion.4), channel_id=1, replica_groups=mesh['zh'=4,'x'=4,'zl'=2,'y'=8,'core'=2] {'zh'}, dimensions={0}, use_global_device_ids=true | all-gather | bytes 737280 | tf_op jit(solution)/shard_map/all_gather | solution.py:38
  113.5 43.5 %all-gather.2.cloned.1.call-done = bf16[384,3072]{1,0:T(8,128)(2,1)} async-done(((bf16[96,3072]{1,0:T(8,128)(2,1)}), bf16[384,3072]{1,0:T(8,128)(2,1)}) %all-gather.2.cloned.1.call-update) | async-done | bytes 2359312 | tf_op jit(solution)/shard_map/all_gather | solution.py:38
  156.9 1.7 fusion.8
  158.7 1.7 fusion.3
  160.6 1.2 slice.94
  161.8 0.2 dot_general.43
  161.9 0.6 convolution_convert_fusion.6
  162.6 1.2 copy.18
  163.9 8.7 %all-to-all-start.3 = ((bf16[32,12,768]{2,1,0:T(8,128)(2,1)}), bf16[32,12,768]{2,1,0:T(8,128)(2,1)S(1)}, u32[]{:S(2)}, u32[]{:S(2)}) async-start(bf16[32,12,768]{2,1,0:T(8,128)(2,1)} %copy.18), calls=%async_computation.3 | async-start | bytes 1572864 | tf_op jit(solution)/shard_map/all_to_all | solution.py:91
  172.5 1.7 fusion
  174.2 1.7 fusion.1
  176.0 1.3 pad_maximum_fusion.1
  177.3 2.7 %fusion.2 = bf16[1,1024,384]{2,1,0:T(8,128)(2,1)} fusion(bf16[384,768]{1,0:T(8,128)(2,1)S(1)} %reshape.84, bf16[384,3072]{1,0:T(8,128)(2,1)} %all-gather.2.cloned.1.call-done), kind=kOutput, calls=%fused_computation.10 | convolution fusion | flops 302383104 | bytes 1867776 | tf_op jit(solution)/shard_map/dot_general | solution.py:21
  180.0 13.8 %all-to-all-done.3 = bf16[32,12,768]{2,1,0:T(8,128)(2,1)S(1)} async-done(((bf16[32,12,768]{2,1,0:T(8,128)(2,1)}), bf16[32,12,768]{2,1,0:T(8,128)(2,1)S(1)}, u32[]{:S(2)}, u32[]{:S(2)}) %all-to-all-start.3) | async-done | bytes 589856 | tf_op jit(solution)/shard_map/all_to_all | solution.py:91
  193.8 0.1 reshape.86
  193.9 0.4 fusion.20
  194.3 0.7 slice.159
  195.0 0.8 fusion.21
  (16 shorter events, 0.5 us)
Async XLA Ops:
  7.2 38.5 %copy-start = (bf16[1,1024,384]{2,1,0:T(8,128)(2,1)S(1)}, bf16[1,1024,384]{2,1,0:T(8,128)(2,1)}, u32[]{:S(2)}) copy-start(bf16[1,1024,384]{2,1,0:T(8,128)(2,1)} %param.11) | copy-start | bytes 2359300
  7.2 149.8 %all-gather.2.cloned.1.call-start = ((), (), s32[]{:S(2)}) async-start(), calls=%async_computation.4 | async-start | bytes 2949120 | tf_op jit(solution)/shard_map/all_gather | solution.py:38
  43.3 1.8 copy-start.2
  163.9 29.9 %all-to-all-start.3 = ((bf16[32,12,768]{2,1,0:T(8,128)(2,1)}), bf16[32,12,768]{2,1,0:T(8,128)(2,1)S(1)}, u32[]{:S(2)}, u32[]{:S(2)}) async-start(bf16[32,12,768]{2,1,0:T(8,128)(2,1)} %copy.18), calls=%async_computation.3 | async-start | bytes 1572864 | tf_op jit(solution)/shard_map/all_to_all | solution.py:91
  180.0 15.0 %copy-start.1 = (f32[192]{0:T(256)S(1)}, f32[192]{0:T(256)}, u32[]{:S(2)}) copy-start(f32[192]{0:T(256)} %param.8) | copy-start | bytes 2308
Sparse Core Ops, SparseCore 0:
  113.6 43.3 all-gather.1

commit v2 on v1

v2 whole, which is shorter than its diff:
```python
import jax
import jax.numpy as jnp
from jax import lax
from jax.sharding import Mesh, PartitionSpec as P

NX = 4
NZ = 4
EXPERTS = 32
TOKEN_AXES = ("zl", "y", "core")


def dot(a, b, dims):
    return lax.dot_general(a, b, (dims, ((), ())), preferred_element_type=jnp.float32)


def half(a):
    return a.astype(jnp.bfloat16)


def dispatch_rows(expert_of, room):
    index = jnp.arange(expert_of.shape[0], dtype=jnp.int32)
    earlier = (expert_of[:, None] == expert_of[None, :]) & (index[None, :] < index[:, None])
    base = expert_of * (2 * room) + jnp.sum(earlier.astype(jnp.int32), axis=1)
    slot = jnp.concatenate([base, base + room])
    rows = jnp.arange(EXPERTS * 2 * room, dtype=jnp.int32)
    return half(slot[None, :] == rows[:, None])


def kind_rows(room):
    rows = jnp.arange(EXPERTS * 2 * room, dtype=jnp.int32)
    kind = rows // (EXPERTS * room)
    expert = (rows // room) % EXPERTS
    column = expert * (2 * room) + kind * room + rows % room
    return half(column[:, None] == rows[None, :])


def exchange(values, axes, parts):
    rows, width = values.shape
    return lax.all_to_all(values.reshape(parts, rows // parts, width), axes, 0, 0, tiled=True)


def add_up(blocks):
    b = [blocks[i].astype(jnp.float32) for i in range(blocks.shape[0])]
    return (b[0] + b[1]) + (b[2] + b[3])


def scatter_sum(partial):
    first = half(add_up(exchange(partial, "x", NX)))
    return add_up(exchange(first, "zh", NZ))


def gather_rows(piece):
    wide = lax.all_gather(piece, "zh", axis=0, tiled=True)
    part, width = wide.shape
    copies = jnp.broadcast_to(wide[None], (NX, part, width))
    return lax.all_to_all(copies, "x", 0, 0, tiled=True).reshape(NX * part, width)


def shards(tokens, expert_of, router_weight, cotangent, gate_up_weight, down_weight):
    tok, feat = tokens.shape
    room = 2 * tok // EXPERTS
    rows = EXPERTS * room
    w_gate = gate_up_weight[0, 0]
    w_up = gate_up_weight[0, 1]
    w_down = down_weight[0]
    ff = w_gate.shape[1]
    scaled = half(router_weight[:, None] * cotangent.astype(jnp.float32))
    dispatch = dispatch_rows(expert_of, room)
    split = kind_rows(room)

    send = half(dot(dispatch, jnp.concatenate([tokens, scaled], axis=0), ((1,), (0,))))
    recv = exchange(send, TOKEN_AXES, EXPERTS).reshape(2 * rows, feat)
    x_rows = half(dot(split[:rows], recv, ((1,), (0,))))
    s_rows = half(dot(split[rows:], recv, ((1,), (0,))))
    total = scatter_sum(
        jnp.concatenate(
            [
                half(dot(x_rows, w_gate, ((1,), (0,)))),
                half(dot(x_rows, w_up, ((1,), (0,)))),
                half(dot(s_rows, w_down, ((1,), (1,)))),
            ],
            axis=1,
        )
    )
    gate = total[:, :ff]
    up = total[:, ff : 2 * ff]
    hidden_grad = total[:, 2 * ff :]
    sig = jax.nn.sigmoid(gate)
    act = gate * sig
    full = gather_rows(
        half(
            jnp.concatenate(
                [
                    act * up,
                    hidden_grad * up * sig * (1.0 + gate * (1.0 - sig)),
                    hidden_grad * act,
                ],
                axis=1,
            )
        )
    )
    hidden = full[:, :ff]
    gate_grad = full[:, ff : 2 * ff]
    up_grad = full[:, 2 * ff :]
    expert_out = half(dot(hidden, w_down, ((1,), (0,))))
    row_grad = half(dot(gate_grad, w_gate, ((1,), (1,))) + dot(up_grad, w_up, ((1,), (1,))))
    back = half(
        dot(split, jnp.concatenate([expert_out, row_grad], axis=0), ((0,), (0,)))
    )
    back = exchange(back, TOKEN_AXES, EXPERTS).reshape(2 * rows, feat)
    grad_gate = half(dot(x_rows, gate_grad, ((0,), (0,))))
    grad_up = half(dot(x_rows, up_grad, ((0,), (0,))))
    grad_down = half(dot(hidden, s_rows, ((0,), (0,))))
    result = dot(dispatch, back, ((0,), (0,)))
    return (
        half(router_weight[:, None] * result[:tok]),
        half(result[tok:]),
        jnp.stack([grad_gate, grad_up])[None],
        grad_down[None],
    )


def solution(mesh):
    fine = Mesh(mesh.devices.reshape(NZ, NX, 2, 8, 2), ("zh", "x", "zl", "y", "core"))
    dp = ("zh", "x")
    ex = TOKEN_AXES
    return jax.shard_map(
        shards,
        mesh=fine,
        in_specs=(P(ex, dp), P(ex), P(ex), P(ex, dp), P(ex, None, dp, None), P(ex, None, dp)),
        out_specs=(P(ex, dp), P(ex, dp), P(ex, None, dp, None), P(ex, None, dp)),
        check_vma=False,
    )
```

time: 204 us -> 173 us (0.85)
  waiting for transfers between devices: 57.3 us -> 31.1 us
  between operations: 14.2 us -> 0.82 us
  starting transfers between devices: 8.69 us -> 19 us
  matrix products: 16.1 us -> 12.9 us
  blocking collectives: 98.1 us -> 101 us
  local copies, waits for them, and re-layouts: 3.8 us -> 1.41 us
    all_gather x1 -> x0, waiting for transfers between devices: 43.5 us -> none  [gather_rows(): lax.all_gather(lax.all_gather(part, 'zh', axis=0, tiled=True), 'x', axis=...]
    all_to_all x1 -> x2, waiting for transfers between devices: 13.8 us -> 31.1 us  [exchange(): lax.all_to_all(values.reshape(parts, rows // parts, width), axes, 0, 0, t...]
    all_to_all x1 -> x2, starting transfers between devices: 8.65 us -> 19 us  [exchange(): lax.all_to_all(values.reshape(parts, rows // parts, width), axes, 0, 0, t...]
    dot_general x12 -> x14, matrix products: 16.1 us -> 12.9 us  [dot(): lax.dot_general(a, b, (dims, ((), ())), preferred_element_type=jnp.float32)]
  transfers between devices with their start and end apart: 2 -> 2, of which waited for: 2 -> 2; matrix products, arithmetic and copies ran while one was open for 4% -> 3% of each run, Pallas kernels for 0% -> 0%
where the time goes in v2:
time: 173 us; the launch traced here: 172 us
  blocking collectives  101 us (58%)
  waiting for transfers between devices  31.1 us (18%)
  starting transfers between devices  19 us (11%)
  matrix products  12.9 us (7%)
  other arithmetic  5.8 us (3%)
    all_to_all x2, blocking collectives, exchange(): lax.all_to_all(values.reshape(parts, rows // parts, width), axes, 0, 0, t...  54.7 us
    all_to_all x2, waiting for transfers between devices, exchange(): lax.all_to_all(values.reshape(parts, rows // parts, width), axes, 0, 0, t...  31.1 us
    all_to_all x1, blocking collectives, gather_rows(): lax.all_to_all(copies, 'x', 0, 0, tiled=True).reshape(NX * part, width)  30 us
    all_to_all x2, starting transfers between devices, exchange(): lax.all_to_all(values.reshape(parts, rows // parts, width), axes, 0, 0, t...  19 us
    all_gather x1, blocking collectives, gather_rows(): wide = lax.all_gather(piece, 'zh', axis=0, tiled=True)  16.2 us
    dot_general x14, matrix products, dot(): lax.dot_general(a, b, (dims, ((), ())), preferred_element_type=jnp.float32)  12.9 us
  transfers between devices with their start and end apart: 2, of which 2 were waited for; matrix products, arithmetic and copies ran while one was open for 3% of the time, Pallas kernels for 0%

profile of v2, /device:TPU:1, one launch (start us, length us, event | category | flops | bytes accessed | tf_op | source)
XLA Modules:
  0.0 172.0 jit_solution(6570759136850809946)
XLA Ops:
  0.6 0.9 convert_reduce_fusion
  1.6 0.7 broadcast_add_fusion
  2.4 1.0 multiply_convert_fusion
  3.4 2.2 %convolution_convert_fusion.6 = bf16[768,384]{1,0:T(8,128)(2,1)} fusion(s32[384]{0:T(512)S(1)} %pad_add_fusion, bf16[192,384]{1,0:T(8,128)(2,1)S(1)} %multiply_convert_fusion, bf16[192,384]{1,0:T(8,128)(2,1)} %param.6), kind=kOutput, calls=%fused_computation.9 | convolution fusion | flops 227672064 | bytes 886272 | tf_op jit(solution)/shard_map/dot_general | solution.py:13
  5.6 10.6 %all-to-all-start = ((bf16[32,24,384]{2,1,0:T(8,128)(2,1)}), bf16[32,24,384]{2,1,0:T(8,128)(2,1)S(1)}, u32[]{:S(2)}, u32[]{:S(2)}) async-start(bf16[32,24,384]{2,1,0:T(8,128)(2,1)} %bitcast), calls=%async_computation | async-start | bytes 1179648 | tf_op jit(solution)/shard_map/all_to_all | solution.py:39
  16.2 0.4 iota_compare_fusion
  16.6 17.4 %all-to-all-done = bf16[32,24,384]{2,1,0:T(8,128)(2,1)S(1)} async-done(((bf16[32,24,384]{2,1,0:T(8,128)(2,1)}), bf16[32,24,384]{2,1,0:T(8,128)(2,1)S(1)}, u32[]{:S(2)}, u32[]{:S(2)}) %all-to-all-start) | async-done | bytes 589856 | tf_op jit(solution)/shard_map/all_to_all | solution.py:39
  34.0 0.5 convolution_convert_fusion.10
  34.4 0.5 convolution_convert_fusion.9
  34.9 0.4 copy-done.4
  35.4 0.6 convolution_convert_fusion.4
  35.9 0.6 convolution_convert_fusion.5
  36.5 0.6 convolution_convert_fusion.3
  37.3 30.7 %all_to_all.25 = bf16[4,96,3072]{2,1,0:T(8,128)(2,1)S(1)} all-to-all(bf16[4,96,3072]{2,1,0:T(8,128)(2,1)S(1)} %bitcast.41), channel_id=1, replica_groups=mesh['zh'=4,'x'=4,'zl'=2,'y'=8,'core'=2] {'x'}, dimensions={0} | all-to-all | bytes 4718592 | tf_op jit(solution)/shard_map/all_to_all | solution.py:39
  68.0 0.3 add_convert_fusion
  68.3 24.0 %all_to_all.26 = bf16[4,24,3072]{2,1,0:T(8,128)(2,1)S(1)} all-to-all(bf16[4,24,3072]{2,1,0:T(8,128)(2,1)S(1)} %bitcast.48), channel_id=1, replica_groups=mesh['zh'=4,'x'=4,'zl'=2,'y'=8,'core'=2] {'zh'}, dimensions={0} | all-to-all | bytes 1179648 | tf_op jit(solution)/shard_map/all_to_all | solution.py:39
  92.5 16.2 %all_gather.3 = bf16[96,3072]{1,0:T(8,128)(2,1)S(1)} all-gather(bf16[24,3072]{1,0:T(8,128)(2,1)S(1)} %pad_maximum_fusion.1), channel_id=1, replica_groups=mesh['zh'=4,'x'=4,'zl'=2,'y'=8,'core'=2] {'zh'}, dimensions={0}, use_global_device_ids=true | all-gather | bytes 737280 | tf_op jit(solution)/shard_map/all_gather | solution.py:53
  108.7 0.3 broadcast_in_dim.6
  109.0 30.0 %all_to_all.27 = bf16[4,96,3072]{2,1,0:T(8,128)(2,1)S(1)} all-to-all(bf16[4,96,3072]{2,1,0:T(8,128)(2,1)S(1)} %broadcast_in_dim.6), channel_id=1, replica_groups=mesh['zh'=4,'x'=4,'zl'=2,'y'=8,'core'=2] {'x'}, dimensions={0} | all-to-all | bytes 4718592 | tf_op jit(solution)/shard_map/all_to_all | solution.py:56
  139.0 0.6 convolution_convert_fusion.8
  139.6 0.6 fusion.11
  140.2 0.6 fusion.3
  140.8 1.8 %convolution_convert_fusion.7 = bf16[768,384]{1,0:T(8,128)(2,1)} fusion(bf16[384,384]{1,0:T(8,128)(2,1)S(1)} %fusion.3, bf16[384,384]{1,0:T(8,128)(2,1)S(1)} %convolution_convert_fusion.8, s32[768]{0:T(1024)S(1)} %fusion.43), kind=kOutput, calls=%fused_computation.10 | convolution fusion | flops 455049216 | bytes 1182720 | tf_op jit(solution)/shard_map/dot_general | solution.py:13
  142.6 8.5 %all-to-all-start.4 = ((bf16[32,24,384]{2,1,0:T(8,128)(2,1)}), bf16[32,24,384]{2,1,0:T(8,128)(2,1)}, u32[]{:S(2)}, u32[]{:S(2)}) async-start(bf16[32,24,384]{2,1,0:T(8,128)(2,1)} %bitcast.49), calls=%async_computation.4 | async-start | bytes 1179648 | tf_op jit(solution)/shard_map/all_to_all | solution.py:39
  151.1 0.6 fusion
  151.7 0.6 fusion.1
  152.3 1.3 maximum_bitcast_fusion
  153.6 1.6 fusion.2
  155.2 13.8 %all-to-all-done.4 = bf16[32,24,384]{2,1,0:T(8,128)(2,1)} async-done(((bf16[32,24,384]{2,1,0:T(8,128)(2,1)}), bf16[32,24,384]{2,1,0:T(8,128)(2,1)}, u32[]{:S(2)}, u32[]{:S(2)}) %all-to-all-start.4) | async-done | bytes 589856 | tf_op jit(solution)/shard_map/all_to_all | solution.py:39
  168.9 1.6 fusion.4
  170.5 0.7 slice.153
  171.2 0.8 fusion.29
  (15 shorter events, 0.4 us)
Async XLA Ops:
  0.6 35.9 %copy-start = (bf16[1,1024,384]{2,1,0:T(8,128)(2,1)S(1)}, bf16[1,1024,384]{2,1,0:T(8,128)(2,1)}, u32[]{:S(2)}) copy-start(bf16[1,1024,384]{2,1,0:T(8,128)(2,1)} %param.11) | copy-start | bytes 2359300
  5.6 28.4 %all-to-all-start = ((bf16[32,24,384]{2,1,0:T(8,128)(2,1)}), bf16[32,24,384]{2,1,0:T(8,128)(2,1)S(1)}, u32[]{:S(2)}, u32[]{:S(2)}) async-start(bf16[32,24,384]{2,1,0:T(8,128)(2,1)} %bitcast), calls=%async_computation | async-start | bytes 1179648 | tf_op jit(solution)/shard_map/all_to_all | solution.py:39
  34.0 1.4 copy-start.4
  35.4 1.2 copy-start.1
  142.6 26.3 %all-to-all-start.4 = ((bf16[32,24,384]{2,1,0:T(8,128)(2,1)}), bf16[32,24,384]{2,1,0:T(8,128)(2,1)}, u32[]{:S(2)}, u32[]{:S(2)}) async-start(bf16[32,24,384]{2,1,0:T(8,128)(2,1)} %bitcast.49), calls=%async_computation.4 | async-start | bytes 1179648 | tf_op jit(solution)/shard_map/all_to_all | solution.py:39
  152.3 1.3 copy-start.2
  153.6 17.6 %copy-start.3 = (f32[192]{0:T(256)S(1)}, f32[192]{0:T(256)}, u32[]{:S(2)}) copy-start(f32[192]{0:T(256)} %param.8) | copy-start | bytes 2308

commit v3 on v2

--- a/solution.py
+++ b/solution.py
@@ -26,12 +26,16 @@
     return half(slot[None, :] == rows[:, None])
 
 
-def kind_rows(room):
-    rows = jnp.arange(EXPERTS * 2 * room, dtype=jnp.int32)
-    kind = rows // (EXPERTS * room)
-    expert = (rows // room) % EXPERTS
-    column = expert * (2 * room) + kind * room + rows % room
-    return half(column[:, None] == rows[None, :])
+def kind_rows(room, kept):
+    rows = jnp.arange(EXPERTS * 2 * kept, dtype=jnp.int32)
+    kind = rows // (EXPERTS * kept)
+    expert = (rows // kept) % EXPERTS
+    column = expert * (2 * room) + kind * room + rows % kept
+    return one_hot(column, EXPERTS * 2 * room)
+
+
+def one_hot(column, width):
+    return half(column[:, None] == jnp.arange(width, dtype=jnp.int32)[None, :])
 
 
 def exchange(values, axes, parts):
@@ -56,20 +60,10 @@
     return lax.all_to_all(copies, "x", 0, 0, tiled=True).reshape(NX * part, width)
 
 
-def shards(tokens, expert_of, router_weight, cotangent, gate_up_weight, down_weight):
-    tok, feat = tokens.shape
-    room = 2 * tok // EXPERTS
-    rows = EXPERTS * room
-    w_gate = gate_up_weight[0, 0]
-    w_up = gate_up_weight[0, 1]
-    w_down = down_weight[0]
+def expert_rows(recv, w_gate, w_up, w_down, room, kept):
+    rows = EXPERTS * kept
     ff = w_gate.shape[1]
-    scaled = half(router_weight[:, None] * cotangent.astype(jnp.float32))
-    dispatch = dispatch_rows(expert_of, room)
-    split = kind_rows(room)
-
-    send = half(dot(dispatch, jnp.concatenate([tokens, scaled], axis=0), ((1,), (0,))))
-    recv = exchange(send, TOKEN_AXES, EXPERTS).reshape(2 * rows, feat)
+    split = kind_rows(room, kept)
     x_rows = half(dot(split[:rows], recv, ((1,), (0,))))
     s_rows = half(dot(split[rows:], recv, ((1,), (0,))))
     total = scatter_sum(
@@ -107,10 +101,34 @@
     back = half(
         dot(split, jnp.concatenate([expert_out, row_grad], axis=0), ((0,), (0,)))
     )
+    spare = ((0, EXPERTS * (room - kept)), (0, 0))
+    return back, jnp.pad(x_rows, spare), jnp.pad(s_rows, spare), jnp.pad(full, spare)
+
+
+def shards(tokens, expert_of, router_weight, cotangent, gate_up_weight, down_weight):
+    tok, feat = tokens.shape
+    room = 2 * tok // EXPERTS
+    rows = EXPERTS * room
+    w_gate = gate_up_weight[0, 0]
+    w_up = gate_up_weight[0, 1]
+    w_down = down_weight[0]
+    scaled = half(router_weight[:, None] * cotangent.astype(jnp.float32))
+    dispatch = dispatch_rows(expert_of, room)
+    send = half(dot(dispatch, jnp.concatenate([tokens, scaled], axis=0), ((1,), (0,))))
+    recv = exchange(send, TOKEN_AXES, EXPERTS).reshape(2 * rows, feat)
+    mine = lax.axis_index(TOKEN_AXES).astype(jnp.int32)
+    busy = jnp.sum((expert_of == mine).astype(jnp.int32)) > 9
+    back, x_rows, s_rows, full = lax.cond(
+        busy,
+        lambda *a: expert_rows(*a, room, room),
+        lambda *a: expert_rows(*a, room, 9),
+        recv, w_gate, w_up, w_down,
+    )
     back = exchange(back, TOKEN_AXES, EXPERTS).reshape(2 * rows, feat)
-    grad_gate = half(dot(x_rows, gate_grad, ((0,), (0,))))
-    grad_up = half(dot(x_rows, up_grad, ((0,), (0,))))
-    grad_down = half(dot(hidden, s_rows, ((0,), (0,))))
+    ff = w_gate.shape[1]
+    grad_gate = half(dot(x_rows, full[:, ff : 2 * ff], ((0,), (0,))))
+    grad_up = half(dot(x_rows, full[:, 2 * ff :], ((0,), (0,))))
+    grad_down = half(dot(full[:, :ff], s_rows, ((0,), (0,))))
     result = dot(dispatch, back, ((0,), (0,)))
     return (
         half(router_weight[:, None] * result[:tok]),

time: 173 us -> 166 us (0.960)
  blocking collectives: 101 us -> 64.7 us
  waiting for transfers between devices: 31.1 us -> 43.1 us
  local copies, waits for them, and re-layouts: 1.41 us -> 9.58 us
  starting transfers between devices: 19 us -> 25.3 us
  matrix products: 12.9 us -> 14.7 us
    all_to_all x1 -> x0, blocking collectives: 30 us -> none  [gather_rows(): lax.all_to_all(copies, 'x', 0, 0, tiled=True).reshape(NX * part, width)]
    all_to_all x0 -> x1, waiting for transfers between devices: none -> 17.5 us  [gather_rows(): lax.all_to_all(copies, 'x', 0, 0, tiled=True).reshape(NX * part, width)]
    all_to_all x2, blocking collectives: 54.7 us -> 47.5 us  [exchange(): lax.all_to_all(values.reshape(parts, rows // parts, width), axes, 0, 0, t...]
    all_to_all x2, waiting for transfers between devices: 31.1 us -> 25.6 us  [exchange(): lax.all_to_all(values.reshape(parts, rows // parts, width), axes, 0, 0, t...]
    pad x0 -> x3, local copies, waits for them, and re-layouts: none -> 5.03 us  [the longest x1 1.68 us: expert_rows(): jnp.pad(s_rows, spare)]
    all_to_all x0 -> x1, starting transfers between devices: none -> 3.58 us  [gather_rows(): lax.all_to_all(copies, 'x', 0, 0, tiled=True).reshape(NX * part, width)]
    all_to_all x2, starting transfers between devices: 19 us -> 21.8 us  [exchange(): lax.all_to_all(values.reshape(parts, rows // parts, width), axes, 0, 0, t...]
    dot_general x14, matrix products: 12.9 us -> 14.7 us  [dot(): lax.dot_general(a, b, (dims, ((), ())), preferred_element_type=jnp.float32)]
  transfers between devices with their start and end apart: 2 -> 3, of which waited for: 2 -> 3; matrix products, arithmetic and copies ran while one was open for 3% -> 8% of each run, Pallas kernels for 0% -> 0%
where the time goes in v3:
time: 166 us; the launch traced here: 165 us
  blocking collectives  64.7 us (39%)
  waiting for transfers between devices  43.1 us (26%)
  starting transfers between devices  25.3 us (15%)
  matrix products  14.7 us (9%)
  local copies, waits for them, and re-layouts  9.58 us (6%)
  other arithmetic  6.19 us (4%)
    all_to_all x2, blocking collectives, exchange(): lax.all_to_all(values.reshape(parts, rows // parts, width), axes, 0, 0, t...  47.5 us
    all_to_all x2, waiting for transfers between devices, exchange(): lax.all_to_all(values.reshape(parts, rows // parts, width), axes, 0, 0, t...  25.6 us
    all_to_all x2, starting transfers between devices, exchange(): lax.all_to_all(values.reshape(parts, rows // parts, width), axes, 0, 0, t...  21.8 us
    all_to_all x1, waiting for transfers between devices, gather_rows(): lax.all_to_all(copies, 'x', 0, 0, tiled=True).reshape(NX * part, width)  17.5 us
    all_gather x1, blocking collectives, gather_rows(): wide = lax.all_gather(piece, 'zh', axis=0, tiled=True)  17.2 us
    dot_general x14, matrix products, dot(): lax.dot_general(a, b, (dims, ((), ())), preferred_element_type=jnp.float32)  14.7 us
    all_to_all x1, starting transfers between devices, gather_rows(): lax.all_to_all(copies, 'x', 0, 0, tiled=True).reshape(NX * part, width)  3.58 us
  transfers between devices with their start and end apart: 3, of which 3 were waited for; matrix products, arithmetic and copies ran while one was open for 8% of the time, Pallas kernels for 0%

profile of v3, /device:TPU:1, one launch (start us, length us, event | category | flops | bytes accessed | tf_op | source)
XLA Modules:
  0.0 165.2 jit_solution(6009056861266144516)
XLA Ops:
  0.6 0.9 convert_reduce_fusion
  1.6 1.3 broadcast_add_fusion
  3.0 1.0 multiply_convert_fusion.6
  4.0 2.2 %convolution_convert_fusion.15 = bf16[768,384]{1,0:T(8,128)(2,1)} fusion(s32[384]{0:T(512)S(1)} %pad_add_fusion, bf16[192,384]{1,0:T(8,128)(2,1)S(1)} %multiply_convert_fusion.6, bf16[192,384]{1,0:T(8,128)(2,1)} %param.8), kind=kOutput, calls=%fused_computation.110 | convolution fusion | flops 227672064 | bytes 886272 | tf_op jit(solution)/shard_map/dot_general | solution.py:13
  6.2 10.6 %all-to-all-start.6 = ((bf16[32,24,384]{2,1,0:T(8,128)(2,1)}), bf16[32,24,384]{2,1,0:T(8,128)(2,1)S(1)}, u32[]{:S(2)}, u32[]{:S(2)}) async-start(bf16[32,24,384]{2,1,0:T(8,128)(2,1)} %bitcast.8), calls=%async_computation.6 | async-start | bytes 1179648 | tf_op jit(solution)/shard_map/all_to_all | solution.py:43
  17.5 1.5 slice_bitcast_fusion
  19.0 15.5 %all-to-all-done.6 = bf16[32,24,384]{2,1,0:T(8,128)(2,1)S(1)} async-done(((bf16[32,24,384]{2,1,0:T(8,128)(2,1)}), bf16[32,24,384]{2,1,0:T(8,128)(2,1)S(1)}, u32[]{:S(2)}, u32[]{:S(2)}) %all-to-all-start.6) | async-done | bytes 589856 | tf_op jit(solution)/shard_map/all_to_all | solution.py:43
  34.6 99.7 %conditional.2 = (bf16[768,384]{1,0:T(8,128)(2,1)}, bf16[384,384]{1,0:T(8,128)(2,1)}, bf16[384,384]{1,0:T(8,128)(2,1)}, bf16[384,3072]{1,0:T(8,128)(2,1)}) conditional(s32[]{:T(128)} %convert_element_type.176, (bf16[768,384]{1,0:T(8,128)(2,1)S(1)}, bf16[384,1024]{1,0:T(8,128)(2,1)S(1)}, bf16[384,1024]{1,0:T(8,128)(2,1)S(1)}, ...), branch_computations={%region_2.3_spmd, %region_3.4_spmd} | conditional | flops 2732974848 | bytes 48249784
  35.8 0.5 convolution_convert_fusion.1
  36.8 0.5 convolution_convert_fusion
  37.4 24.4 %all_to_all.34 = bf16[4,72,3072]{2,1,0:T(8,128)(2,1)S(1)} all-to-all(bf16[4,72,3072]{2,1,0:T(8,128)(2,1)S(1)} %bitcast.59), channel_id=1, replica_groups=mesh['zh'=4,'x'=4,'zl'=2,'y'=8,'core'=2] {'x'}, dimensions={0} | all-to-all | bytes 3538944 | tf_op jit(solution)/shard_map/cond/branch_0_fun/all_to_all | solution.py:43
  62.2 23.1 %all_to_all.35 = bf16[4,18,3072]{2,1,0:T(8,128)(2,1)S(1)} all-to-all(bf16[4,18,3072]{2,1,0:T(8,128)(2,1)S(1)} %convert_element_type.139), channel_id=1, replica_groups=mesh['zh'=4,'x'=4,'zl'=2,'y'=8,'core'=2] {'zh'}, dimensions={0} | all-to-all | bytes 884736 | tf_op jit(solution)/shard_map/cond/branch_0_fun/all_to_all | solution.py:43
  85.4 17.2 %all-gather = bf16[4,18,3072]{2,1,0:T(8,128)(2,1)S(1)} all-gather(bf16[1,18,3072]{2,1,0:T(8,128)(2,1)S(1)} %maximum_bitcast_fusion), channel_id=1, replica_groups=mesh['zh'=4,'x'=4,'zl'=2,'y'=8,'core'=2] {'zh'}, dimensions={0}, use_global_device_ids=true | all-gather | bytes 552960 | tf_op jit(solution)/shard_map/cond/branch_0_fun/all_gather | solution.py:57
  102.8 1.4 broadcast_in_dim.0
  104.2 3.6 %all-to-all-start.2 = ((bf16[4,72,3072]{2,1,0:T(8,128)(2,1)}), bf16[4,72,3072]{2,1,0:T(8,128)(2,1)S(1)}, u32[]{:S(2)}, u32[]{:S(2)}) async-start(bf16[4,72,3072]{2,1,0:T(8,128)(2,1)} %broadcast_in_dim.0), calls=%async_computation.2 | async-start | bytes 3538944 | tf_op jit(solution)/shard_map/cond/branch_0_fun/all_to_all | solution.py:60
  107.8 1.7 %pad.9 = bf16[384,384]{1,0:T(8,128)(2,1)} pad(bf16[288,384]{1,0:T(8,128)(2,1)} %copy-done.4, bf16[]{:T(256)} %constant.94.clone), padding=0_96x0_0 | pad | bytes 516098 | tf_op jit(solution)/shard_map/cond/branch_0_fun/jit(_pad)/pad | solution.py:105
  109.5 1.7 %pad.8 = bf16[384,384]{1,0:T(8,128)(2,1)} pad(bf16[288,384]{1,0:T(8,128)(2,1)} %copy-done.3, bf16[]{:T(256)} %constant.94.clone), padding=0_96x0_0 | pad | bytes 516098 | tf_op jit(solution)/shard_map/cond/branch_0_fun/jit(_pad)/pad | solution.py:105
  111.1 17.5 %all-to-all-done.2 = bf16[4,72,3072]{2,1,0:T(8,128)(2,1)S(1)} async-done(((bf16[4,72,3072]{2,1,0:T(8,128)(2,1)}), bf16[4,72,3072]{2,1,0:T(8,128)(2,1)S(1)}, u32[]{:S(2)}, u32[]{:S(2)}) %all-to-all-start.2) | async-done | bytes 1769504 | tf_op jit(solution)/shard_map/cond/branch_0_fun/all_to_all | solution.py:60
  128.7 0.5 fusion.4
  129.2 0.6 copy-done.2
  130.3 1.7 %pad.10 = bf16[384,3072]{1,0:T(8,128)(2,1)} pad(bf16[288,3072]{1,0:T(8,128)(2,1)S(1)} %bitcast.56, bf16[]{:T(256)} %constant.94.clone), padding=0_96x0_0 | pad | bytes 4128770 | tf_op jit(solution)/shard_map/cond/branch_0_fun/jit(_pad)/pad | solution.py:105
  132.0 0.5 fusion
  132.5 1.8 %fusion.7 = bf16[768,384]{1,0:T(8,128)(2,1)} fusion(bf16[288,384]{1,0:T(8,128)(2,1)S(1)} %fusion, bf16[288,384]{1,0:T(8,128)(2,1)S(1)} %convolution_convert_fusion.3, s32[576]{0:T(1024)S(1)} %fusion.20), kind=kOutput, calls=%fused_computation.17 | convolution fusion | flops 341065728 | bytes 1034496 | tf_op jit(solution)/shard_map/cond/branch_0_fun/dot_general | solution.py:13
  134.2 11.2 %all-to-all-start.7 = ((bf16[32,24,384]{2,1,0:T(8,128)(2,1)}), bf16[32,24,384]{2,1,0:T(8,128)(2,1)S(1)}, u32[]{:S(2)}, u32[]{:S(2)}) async-start(bf16[32,24,384]{2,1,0:T(8,128)(2,1)} %bitcast.13), calls=%async_computation.7 | async-start | bytes 1179648 | tf_op jit(solution)/shard_map/all_to_all | solution.py:43
  145.5 1.8 %fusion.55 = bf16[1,384,1024]{2,1,0:T(8,128)(2,1)S(1)} fusion(bf16[384,384]{1,0:T(8,128)(2,1)} %get-tuple-element.38, bf16[384,3072]{1,0:T(8,128)(2,1)} %get-tuple-element.39), kind=kOutput, calls=%fused_computation.112 | convolution fusion | flops 302383104 | bytes 1867776 | tf_op jit(solution)/shard_map/dot_general | solution.py:13
  147.3 1.8 %fusion.54 = bf16[1,384,1024]{2,1,0:T(8,128)(2,1)S(1)} fusion(bf16[384,384]{1,0:T(8,128)(2,1)} %get-tuple-element.38, bf16[384,3072]{1,0:T(8,128)(2,1)} %get-tuple-element.39), kind=kOutput, calls=%fused_computation.111 | convolution fusion | flops 302383104 | bytes 1867776 | tf_op jit(solution)/shard_map/dot_general | solution.py:13
  149.1 1.3 maximum_bitcast_fusion.1
  150.4 2.8 %fusion.56 = bf16[1,1024,384]{2,1,0:T(8,128)(2,1)} fusion(bf16[384,384]{1,0:T(8,128)(2,1)} %get-tuple-element.40, bf16[384,3072]{1,0:T(8,128)(2,1)} %get-tuple-element.39), kind=kOutput, calls=%fused_computation.113 | convolution fusion | flops 302383104 | bytes 1867776 | tf_op jit(solution)/shard_map/dot_general | solution.py:13
  153.2 10.1 %all-to-all-done.7 = bf16[32,24,384]{2,1,0:T(8,128)(2,1)S(1)} async-done(((bf16[32,24,384]{2,1,0:T(8,128)(2,1)}), bf16[32,24,384]{2,1,0:T(8,128)(2,1)S(1)}, u32[]{:S(2)}, u32[]{:S(2)}) %all-to-all-start.7) | async-done | bytes 589856 | tf_op jit(solution)/shard_map/all_to_all | solution.py:43
  163.2 0.5 fusion.57
  163.8 0.7 slice.227
  164.4 0.8 fusion.63
  (25 shorter events, 3.0 us)
Async XLA Ops:
  6.2 28.4 %all-to-all-start.6 = ((bf16[32,24,384]{2,1,0:T(8,128)(2,1)}), bf16[32,24,384]{2,1,0:T(8,128)(2,1)S(1)}, u32[]{:S(2)}, u32[]{:S(2)}) async-start(bf16[32,24,384]{2,1,0:T(8,128)(2,1)} %bitcast.8), calls=%async_computation.6 | async-start | bytes 1179648 | tf_op jit(solution)/shard_map/all_to_all | solution.py:43
  16.8 17.8 %copy-start = (bf16[1,1024,384]{2,1,0:T(8,128)(2,1)S(1)}, bf16[1,1024,384]{2,1,0:T(8,128)(2,1)}, u32[]{:S(2)}) copy-start(bf16[1,1024,384]{2,1,0:T(8,128)(2,1)} %param.13) | copy-start | bytes 2359300
  34.6 2.2 %copy-start.1 = (bf16[1024,384]{1,0:T(8,128)(2,1)}, bf16[1024,384]{1,0:T(8,128)(2,1)S(1)}, u32[]{:S(2)}) copy-start(bf16[1024,384]{1,0:T(8,128)(2,1)S(1)} %get-tuple-element.24) | copy-start | bytes 2359300 | tf_op jit(solution)/shard_map/conditional
  35.3 1.4 copy-start.3
  35.8 1.0 copy-start.4
  104.2 24.5 %all-to-all-start.2 = ((bf16[4,72,3072]{2,1,0:T(8,128)(2,1)}), bf16[4,72,3072]{2,1,0:T(8,128)(2,1)S(1)}, u32[]{:S(2)}, u32[]{:S(2)}) async-start(bf16[4,72,3072]{2,1,0:T(8,128)(2,1)} %broadcast_in_dim.0), calls=%async_computation.2 | async-start | bytes 3538944 | tf_op jit(solution)/shard_map/cond/branch_0_fun/all_to_all | solution.py:60
  128.7 1.1 copy-start.2
  134.2 29.0 %all-to-all-start.7 = ((bf16[32,24,384]{2,1,0:T(8,128)(2,1)}), bf16[32,24,384]{2,1,0:T(8,128)(2,1)S(1)}, u32[]{:S(2)}, u32[]{:S(2)}) async-start(bf16[32,24,384]{2,1,0:T(8,128)(2,1)} %bitcast.13), calls=%async_computation.7 | async-start | bytes 1179648 | tf_op jit(solution)/shard_map/all_to_all | solution.py:43
  150.4 14.1 %copy-start.5 = (f32[192]{0:T(256)S(1)}, f32[192]{0:T(256)}, u32[]{:S(2)}) copy-start(f32[192]{0:T(256)} %param.10) | copy-start | bytes 2308

commit v4 on v2

v4 whole, which is shorter than its diff:
```python
import jax
import jax.numpy as jnp
from jax import lax
from jax.experimental import pallas as pl
from jax.experimental.pallas import tpu as pltpu
from jax.sharding import Mesh, PartitionSpec as P

NX = 4
NZ = 4
EXPERTS = 32
TOKEN_AXES = ("zl", "y", "core")
VMEM_BYTES = 56 * 1024 * 1024


def dot(a, b, dims):
    return lax.dot_general(a, b, (dims, ((), ())), preferred_element_type=jnp.float32)


def half(a):
    return a.astype(jnp.bfloat16)


def kernel_call(body, outs, *args):
    whole = pl.BlockSpec(memory_space=pltpu.VMEM)
    return pl.pallas_call(
        body,
        out_shape=[jax.ShapeDtypeStruct(shape, dtype) for shape, dtype in outs],
        in_specs=[whole] * len(args),
        out_specs=[whole] * len(outs),
        compiler_params=pltpu.CompilerParams(vmem_limit_bytes=VMEM_BYTES),
    )(*args)


def as_column(row):
    n = row.shape[1]
    eye = lax.broadcasted_iota(jnp.int32, (n, n), 0) == lax.broadcasted_iota(jnp.int32, (n, n), 1)
    return jnp.sum(jnp.where(eye, row, 0.0), axis=1, keepdims=True)


def where_one(mask):
    return half(jnp.where(mask, 1.0, 0.0))


def iota(shape, dim):
    return lax.broadcasted_iota(jnp.int32, shape, dim)


COUNT_LANES = 128
MAIN = 8
REST = 4
BLOCK_ROWS = EXPERTS * MAIN


def send_body(expert_ref, weight_ref, tokens_ref, cotangent_ref, send_ref):
    expert = expert_ref[...].astype(jnp.float32)
    n = expert.shape[1]
    feat = tokens_ref.shape[1]
    column = as_column(expert)
    same = (column == expert) & (iota((n, n), 0) < iota((n, n), 1))
    position = jnp.sum(jnp.where(same, 1.0, 0.0), axis=0, keepdims=True)
    slot = (expert * MAIN + position).astype(jnp.int32)
    main = jnp.where(position < MAIN, slot, -1)
    rest = jnp.where(position < MAIN, -MAIN, slot - MAIN)
    rows = iota((BLOCK_ROWS, n), 0)
    scaled = half(as_column(weight_ref[...]) * cotangent_ref[...].astype(jnp.float32))
    tokens = tokens_ref[...]
    pick = where_one(rows == main)
    send_ref[:, :feat] = half(dot(pick, tokens, ((1,), (0,))))
    send_ref[:, feat : 2 * feat] = half(dot(pick, scaled, ((1,), (0,))))
    named = jnp.where(jnp.right_shift(rows, 3) == expert_ref[...], 1.0, 0.0)
    counts = jnp.sum(named, axis=1, keepdims=True)
    send_ref[:, 3 * feat :] = half(jnp.broadcast_to(counts, (BLOCK_ROWS, COUNT_LANES)))
    send_ref[:, 2 * feat : 3 * feat] = half(
        dot(where_one(rows == rest), tokens, ((1,), (0,)))
        + dot(where_one(rows == rest + REST), scaled, ((1,), (0,)))
    )


def result_body(expert_ref, weight_ref, back_ref, out_ref, grad_ref):
    expert = expert_ref[...].astype(jnp.float32)
    n = expert.shape[1]
    feat = out_ref.shape[1]
    column = as_column(expert)
    same = (column == expert) & (iota((n, n), 1) < iota((n, n), 0))
    position = jnp.sum(jnp.where(same, 1.0, 0.0), axis=1, keepdims=True)
    slot = (column * MAIN + position).astype(jnp.int32)
    main = jnp.where(position < MAIN, slot, -1)
    rest = jnp.where(position < MAIN, -MAIN, slot - MAIN)
    columns = iota((n, BLOCK_ROWS), 1)
    pick = where_one(columns == main)
    last = back_ref[:, 2 * feat :]
    out = dot(pick, back_ref[:, :feat], ((1,), (0,))) + dot(
        where_one(columns == rest), last, ((1,), (0,))
    )
    grad = dot(pick, back_ref[:, feat : 2 * feat], ((1,), (0,))) + dot(
        where_one(columns == rest + REST), last, ((1,), (0,))
    )
    out_ref[...] = half(as_column(weight_ref[...]) * out)
    grad_ref[...] = half(grad)


def row_targets(counts):
    n = BLOCK_ROWS
    above = iota((n, n), 0)
    across = iota((n, n), 1)
    count = jnp.sum(jnp.where(above == across, counts, 0.0), axis=0, keepdims=True)
    earlier = jnp.right_shift(above, 3) < jnp.right_shift(across, 3)
    heads = (jnp.bitwise_and(above, MAIN - 1) == 0) & earlier
    offset = jnp.sum(jnp.where(heads, counts, 0.0), axis=0, keepdims=True)
    count = count.astype(jnp.int32)
    offset = offset.astype(jnp.int32)
    lane = jnp.bitwise_and(iota((1, n), 1), MAIN - 1)
    tail = MAIN + jnp.bitwise_and(lane, REST - 1)
    held = tail < count
    return (
        jnp.where(lane < count, offset + lane, -1),
        jnp.where(held & (lane < REST), offset + tail, -1),
        jnp.where(held & (lane >= REST), offset + tail, -1),
    )


def partial_body(recv_ref, w_gu_ref, w_down_ref, x_ref, s_ref, target_ref, partial_ref):
    part = partial_ref.shape[2]
    rows = NX * part
    room = x_ref.shape[0] // NX
    feat = x_ref.shape[1]
    quarter = w_down_ref.shape[0] // NZ
    index = iota((rows, BLOCK_ROWS), 0)
    targets = row_targets(recv_ref[:, 3 * feat : 3 * feat + 1].astype(jnp.float32))
    for k in range(3):
        target_ref[k : k + 1, :] = targets[k]
    pick = where_one(index == targets[0])
    last = recv_ref[:, 2 * feat : 3 * feat]
    x_rows = half(
        dot(pick, recv_ref[:, :feat], ((1,), (0,)))
        + dot(where_one(index == targets[1]), last, ((1,), (0,)))
    )
    s_rows = half(
        dot(pick, recv_ref[:, feat : 2 * feat], ((1,), (0,)))
        + dot(where_one(index == targets[2]), last, ((1,), (0,)))
    )
    for ref, values in ((x_ref, x_rows), (s_ref, s_rows)):
        for x in range(NX):
            ref[x * room : x * room + part, :] = values[x * part : (x + 1) * part]
            if part < room:
                ref[x * room + part : (x + 1) * room, :] = jnp.zeros(
                    (room - part, feat), values.dtype
                )
    for q in range(NZ):
        cols = slice(q * quarter, (q + 1) * quarter)
        products = (
            dot(x_rows, w_gu_ref[0, 0, :, cols], ((1,), (0,))),
            dot(x_rows, w_gu_ref[0, 1, :, cols], ((1,), (0,))),
            dot(s_rows, w_down_ref[cols, :], ((1,), (1,))),
        )
        for k, product in enumerate(products):
            for x in range(NX):
                partial_ref[x, q, :, k * quarter : (k + 1) * quarter] = half(
                    product[x * part : (x + 1) * part]
                )


def back_body(full_ref, target_ref, w_gu_ref, w_down_ref, back_ref, *padded_refs):
    part = full_ref.shape[2]
    rows = NX * part
    quarter = w_down_ref.shape[0] // NZ
    feat = w_down_ref.shape[1]
    out = jnp.zeros((rows, feat), jnp.float32)
    grad = jnp.zeros((rows, feat), jnp.float32)
    for q in range(NZ):
        cols = slice(q * quarter, (q + 1) * quarter)

        def values(k):
            return full_ref[:, q, :, k * quarter : (k + 1) * quarter].reshape(rows, quarter)

        out += dot(values(0), w_down_ref[cols, :], ((1,), (0,)))
        grad += dot(values(1), w_gu_ref[0, 0, :, cols], ((1,), (1,)))
        grad += dot(values(2), w_gu_ref[0, 1, :, cols], ((1,), (1,)))
    out = half(out)
    grad = half(grad)
    index = iota((rows, BLOCK_ROWS), 0)
    pick = where_one(index == target_ref[0:1, :])
    back_ref[:, :feat] = half(dot(pick, out, ((0,), (0,))))
    back_ref[:, feat : 2 * feat] = half(dot(pick, grad, ((0,), (0,))))
    back_ref[:, 2 * feat :] = half(
        dot(where_one(index == target_ref[1:2, :]), out, ((0,), (0,)))
        + dot(where_one(index == target_ref[2:3, :]), grad, ((0,), (0,)))
    )
    for ref in padded_refs:
        ref[:, :, :part, :] = full_ref[...]
        room = ref.shape[2]
        ref[:, :, part:, :] = jnp.zeros(ref.shape[:2] + (room - part, ref.shape[3]), ref.dtype)


def add_up(blocks):
    b = [blocks[i].astype(jnp.float32) for i in range(blocks.shape[0])]
    return (b[0] + b[1]) + (b[2] + b[3])


LEVELS = (192, 224, 288, 384)


def expert_rows(recv, w_gu, w_down, rows):
    full_rows = LEVELS[-1]
    part = rows // NX
    ff, feat = w_down.shape
    quarter = ff // NZ
    bf = jnp.bfloat16
    x_rows, s_rows, target, partial = kernel_call(
        partial_body,
        [
            ((full_rows, feat), bf),
            ((full_rows, feat), bf),
            ((3, BLOCK_ROWS), jnp.int32),
            ((NX, NZ, part, 3 * quarter), bf),
        ],
        recv, w_gu, w_down,
    )
    first = half(add_up(lax.all_to_all(partial, "x", 0, 0, tiled=True)))
    total = add_up(lax.all_to_all(first, "zh", 0, 0, tiled=True))
    gate = total[:, :quarter]
    up = total[:, quarter : 2 * quarter]
    hidden_grad = total[:, 2 * quarter :]
    sig = jax.nn.sigmoid(gate)
    act = gate * sig
    piece = half(
        jnp.concatenate(
            [
                act * up,
                hidden_grad * up * sig * (1.0 + gate * (1.0 - sig)),
                hidden_grad * act,
            ],
            axis=1,
        )
    )
    wide = lax.all_gather(piece, "zh", axis=0, tiled=True)
    copies = jnp.broadcast_to(
        wide.reshape(1, NZ, part, 3 * quarter), (NX, NZ, part, 3 * quarter)
    )
    full = lax.all_to_all(copies, "x", 0, 0, tiled=True)
    outs = [((BLOCK_ROWS, 3 * feat), bf)]
    if rows < full_rows:
        outs.append(((NX, NZ, full_rows // NX, 3 * quarter), bf))
    back = kernel_call(back_body, outs, full, target, w_gu, w_down)
    return back[0], x_rows, s_rows, back[-1] if rows < full_rows else full


def shards(tokens, expert_of, router_weight, cotangent, gate_up_weight, down_weight):
    tok, feat = tokens.shape
    rows = LEVELS[-1]
    w_down = down_weight[0]
    ff = w_down.shape[0]
    quarter = ff // NZ
    expert_row = expert_of.reshape(1, tok)
    weight_row = router_weight.reshape(1, tok)
    bf = jnp.bfloat16
    (send,) = kernel_call(
        send_body, [((BLOCK_ROWS, 3 * feat + COUNT_LANES), bf)], expert_row, weight_row, tokens, cotangent
    )

    def exchange(values):
        return lax.all_to_all(
            values.reshape(EXPERTS, MAIN, values.shape[1]), TOKEN_AXES, 0, 0, tiled=True
        ).reshape(values.shape)

    recv = exchange(send)
    count = jnp.sum(recv[:, 3 * feat :].astype(jnp.float32)) / (MAIN * COUNT_LANES)
    level = sum((count > limit).astype(jnp.int32) for limit in LEVELS[:-1])
    back, x_rows, s_rows, full = lax.switch(
        level,
        [lambda *a, n=n: expert_rows(*a, n) for n in LEVELS],
        recv, gate_up_weight, w_down,
    )
    back = exchange(back)
    x_parts = x_rows.reshape(NX, rows // NX, feat)
    s_parts = s_rows.reshape(NX, rows // NX, feat)
    grad_gate_up = jnp.einsum(
        "xrd,xqrf->dqf", x_parts, full[..., quarter:], preferred_element_type=jnp.float32
    )
    grad_down = jnp.einsum(
        "xqrf,xrd->qfd", full[..., :quarter], s_parts, preferred_element_type=jnp.float32
    )
    grad_gate = half(grad_gate_up[..., :quarter]).reshape(feat, ff)
    grad_up = half(grad_gate_up[..., quarter:]).reshape(feat, ff)
    layer_out, grad_tokens = kernel_call(
        result_body,
        [((tok, feat), bf), ((tok, feat), bf)],
        expert_row, weight_row, back,
    )
    return (
        layer_out,
        grad_tokens,
        jnp.stack([grad_gate, grad_up])[None],
        half(grad_down).reshape(1, ff, feat),
    )


def solution(mesh):
    fine = Mesh(mesh.devices.reshape(NZ, NX, 2, 8, 2), ("zh", "x", "zl", "y", "core"))
    dp = ("zh", "x")
    ex = TOKEN_AXES
    return jax.shard_map(
        shards,
        mesh=fine,
        in_specs=(P(ex, dp), P(ex), P(ex), P(ex, dp), P(ex, None, dp, None), P(ex, None, dp)),
        out_specs=(P(ex, dp), P(ex, dp), P(ex, None, dp, None), P(ex, None, dp)),
        check_vma=False,
    )
```

time: 173 us -> 155 us (0.90)
  waiting for transfers between devices: 31.1 us -> 9.99 us
  Pallas kernels: 0 us -> 12.4 us
  starting transfers between devices: 19 us -> 30.9 us
  blocking collectives: 101 us -> 90.7 us
  matrix products: 12.9 us -> 5.19 us
  other arithmetic: 5.8 us -> 1.03 us
    all_to_all x2 -> x1, waiting for transfers between devices: 31.1 us -> 9.99 us  [exchange(): lax.all_to_all(values.reshape(EXPERTS, MAIN, values.shape[1]), TOKEN_AXES...]
    pallas_call x0 -> x4, Pallas kernels: none -> 12.4 us  [kernel_call(): pl.pallas_call(body, out_shape=[jax.ShapeDtypeStruct(shape, dtype) for sh...]
    all_to_all x2 -> x1, starting transfers between devices: 19 us -> 30.9 us  [exchange(): lax.all_to_all(values.reshape(EXPERTS, MAIN, values.shape[1]), TOKEN_AXES...]
    dot_general x14 -> x2, matrix products: 12.9 us -> 5.19 us  [the longest x1 2.78 us: shards(): jnp.einsum('xqrf,xrd->qfd', full[..., :quarter], s_parts, preferred_eleme...]
    all_to_all x3 -> x4, blocking collectives: 84.7 us -> 79.3 us  [the longest x1 29.5 us: exchange(): lax.all_to_all(values.reshape(EXPERTS, MAIN, values.shape[1]), TOKEN_AXES...]
    all_gather x1, blocking collectives: 16.2 us -> 11.5 us  [expert_rows(): wide = lax.all_gather(piece, 'zh', axis=0, tiled=True)]
    convert_element_type x3 -> x1, other arithmetic: 2.09 us -> 0.15 us  [half(): return a.astype(jnp.bfloat16)]
  transfers between devices with their start and end apart: 2 -> 1, of which waited for: 2 -> 1; matrix products, arithmetic and copies ran while one was open for 3% -> 5% of each run, Pallas kernels for 0% -> 0%
where the time goes in v4:
time: 155 us; the launch traced here: 154 us
  blocking collectives  90.7 us (59%)
  starting transfers between devices  30.9 us (20%)
  Pallas kernels  12.4 us (8%)
  waiting for transfers between devices  9.99 us (6%)
  matrix products  5.19 us (3%)
  local copies, waits for them, and re-layouts  2.53 us (2%)
    all_to_all x1, starting transfers between devices, exchange(): lax.all_to_all(values.reshape(EXPERTS, MAIN, values.shape[1]), TOKEN_AXES...  30.9 us
    all_to_all x1, blocking collectives, exchange(): lax.all_to_all(values.reshape(EXPERTS, MAIN, values.shape[1]), TOKEN_AXES...  29.5 us
    all_to_all x1, blocking collectives, expert_rows(): first = half(add_up(lax.all_to_all(partial, 'x', 0, 0, tiled=True)))  18.3 us
    all_to_all x1, blocking collectives, expert_rows(): total = add_up(lax.all_to_all(first, 'zh', 0, 0, tiled=True))  17.7 us
    all_to_all x1, blocking collectives, expert_rows(): full = lax.all_to_all(copies, 'x', 0, 0, tiled=True)  13.7 us
    pallas_call x4, Pallas kernels, kernel_call(): pl.pallas_call(body, out_shape=[jax.ShapeDtypeStruct(shape, dtype) for sh...  12.4 us
    all_gather x1, blocking collectives, expert_rows(): wide = lax.all_gather(piece, 'zh', axis=0, tiled=True)  11.5 us
    all_to_all x1, waiting for transfers between devices, exchange(): lax.all_to_all(values.reshape(EXPERTS, MAIN, values.shape[1]), TOKEN_AXES...  9.99 us
  transfers between devices with their start and end apart: 1, of which 1 were waited for; matrix products, arithmetic and copies ran while one was open for 5% of the time, Pallas kernels for 0%

profile of v4, /device:TPU:1, one launch (start us, length us, event | category | flops | bytes accessed | tf_op | source)
XLA Modules:
  0.0 154.2 jit_solution(8740439178341803859)
XLA Ops:
  0.6 0.0 copy-start
  0.6 2.5 %shard_map.93 = bf16[256,1280]{1,0:T(8,128)(2,1)} custom-call(s32[1,192]{1,0:T(1,128)} %bitcast.62, f32[1,192]{1,0:T(1,128)} %bitcast.64, bf16[192,384]{1,0:T(8,128)(2,1)} %tokens_ref.1, bf16[192,384]{1,0:T(8,128)(2,1)} %cotangent_ref.1), custom_call_target="tpu_custom_call" | custom-call | tf_op jit(solution)/shard_map/pallas_call | solution.py:25
  3.2 29.5 %all_to_all.70 = bf16[32,8,1280]{2,1,0:T(8,128)(2,1)S(1)} all-to-all(bf16[32,8,1280]{2,1,0:T(8,128)(2,1)} %bitcast.57), channel_id=1, replica_groups=mesh['zh'=4,'x'=4,'zl'=2,'y'=8,'core'=2] {'zl','y','core'}, dimensions={0} | all-to-all | bytes 1310720 | tf_op jit(solution)/shard_map/all_to_all | solution.py:262
  32.7 0.6 convert_reduce_fusion
  34.0 0.0 copy-done
  34.0 69.1 %conditional.1 = (bf16[256,1152]{1,0:T(8,128)(2,1)}, bf16[384,384]{1,0:T(8,128)(2,1)S(1)}, bf16[384,384]{1,0:T(8,128)(2,1)}, bf16[4,4,96,768]{3,2,1,0:T(8,128)(2,1)}) conditional(s32[]{:T(128)} %clamp.3, (bf16[256,1280]{1,0:T(8,128)(2,1)S(1)}, bf16[1,2,384,1024]{3,2,1,0:T(8,128)(2,1)S(1)}, ...), branch_computations={%region_1.0_spmd, %region_2.0_spmd, %region_3.0_spmd, %region_4.0_... | conditional | flops 3686400 | bytes 22020156 | solution.py:269
  34.0 3.3 %branch_0_fun.2 = (bf16[384,384]{1,0:T(8,128)(2,1)S(1)}, bf16[384,384]{1,0:T(8,128)(2,1)}, s32[3,256]{1,0:T(4,128)}, bf16[4,4,48,768]{3,2,1,0:T(8,128)(2,1)}) custom-call(bf16[256,1280]{1,0:T(8,128)(2,1)S(1)} %get-tuple-element.24.recv_ref, bf16[1,2,384,1024]{3,2,1,0:T(8,128)(2,1)S(1)} %get-tuple-element.25.w_gu_ref, ...), custom_call_target="tpu_custom_call" | custom-call | tf_op jit(solution)/shard_map/cond/branch_0_fun/pallas_call | solution.py:25
  37.3 18.3 %all_to_all.58 = bf16[4,4,48,768]{3,2,1,0:T(8,128)(2,1)S(1)} all-to-all(bf16[4,4,48,768]{3,2,1,0:T(8,128)(2,1)} %get-tuple-element.27), channel_id=1, replica_groups=mesh['zh'=4,'x'=4,'zl'=2,'y'=8,'core'=2] {'x'}, dimensions={0} | all-to-all | bytes 2359296 | tf_op jit(solution)/shard_map/cond/branch_0_fun/all_to_all | solution.py:219
  55.6 0.1 fusion
  55.7 17.7 %all_to_all.59 = bf16[4,48,768]{2,1,0:T(8,128)(2,1)S(1)} all-to-all(bf16[4,48,768]{2,1,0:T(8,128)(2,1)S(1)} %fusion), channel_id=1, replica_groups=mesh['zh'=4,'x'=4,'zl'=2,'y'=8,'core'=2] {'zh'}, dimensions={0} | all-to-all | bytes 589824 | tf_op jit(solution)/shard_map/cond/branch_0_fun/all_to_all | solution.py:220
  73.5 11.5 %all_gather.8 = bf16[192,768]{1,0:T(8,128)(2,1)S(1)} all-gather(bf16[48,768]{1,0:T(8,128)(2,1)S(1)} %pad_maximum_fusion), channel_id=1, replica_groups=mesh['zh'=4,'x'=4,'zl'=2,'y'=8,'core'=2] {'zh'}, dimensions={0}, use_global_device_ids=true | all-gather | bytes 368640 | tf_op jit(solution)/shard_map/cond/branch_0_fun/all_gather | solution.py:236
  85.0 0.0 copy-start.1
  85.0 0.1 broadcast_in_dim.19
  85.1 13.7 %all_to_all.60.full_ref = bf16[4,4,48,768]{3,2,1,0:T(8,128)(2,1)} all-to-all(bf16[4,4,48,768]{3,2,1,0:T(8,128)(2,1)S(1)} %broadcast_in_dim.19), channel_id=1, replica_groups=mesh['zh'=4,'x'=4,'zl'=2,'y'=8,'core'=2] {'x'}, dimensions={0} | all-to-all | bytes 2359296 | tf_op jit(solution)/shard_map/cond/branch_0_fun/all_to_all | solution.py:240
  98.9 0.0 copy-done.1
  98.9 4.2 %branch_0_fun.3 = (bf16[256,1152]{1,0:T(8,128)(2,1)}, bf16[4,4,96,768]{3,2,1,0:T(8,128)(2,1)}) custom-call(bf16[4,4,48,768]{3,2,1,0:T(8,128)(2,1)} %all_to_all.60.full_ref, s32[3,256]{1,0:T(4,128)} %get-tuple-element.28.target_ref, bf16[1,2,384,1024]{3,2,1,0:T(8,128)(2,1)S(1)} %get-tuple-element.25.w_gu_ref, bf16[1024,384]{1,0:T(8,128)(2,1)S(1)} %copy-done.1), custom_call_target="tpu_custom_call" | custom-call | tf_op jit(solution)/shard_map/cond/branch_0_fun/pallas_call | solution.py:25
  103.1 30.9 %all-to-all-start.13 = ((bf16[32,8,1152]{2,1,0:T(8,128)(2,1)}), bf16[32,8,1152]{2,1,0:T(8,128)(2,1)}, u32[]{:S(2)}, u32[]{:S(2)}) async-start(bf16[32,8,1152]{2,1,0:T(8,128)(2,1)} %bitcast.17), calls=%async_computation.13 | async-start | bytes 1179648 | tf_op jit(solution)/shard_map/all_to_all | solution.py:262
  134.0 2.4 %bitcast_convert_fusion = bf16[384,4,512]{2,0,1:T(8,128)(2,1)S(1)} fusion(bf16[4,96,384,1]{2,1,0,3:T(8,128)(2,1)S(1)} %bitcast.66, bf16[4,4,96,768]{3,2,1,0:T(8,128)(2,1)} %get-tuple-element.72), kind=kOutput, calls=%fused_computation.36 | convolution fusion | flops 604766208 | bytes 3440640 | tf_op jit(solution)/shard_map/xrd,xqrf->dqf/dot_general | solution.py:277
  136.4 0.1 fusion.10
  136.5 0.4 copy.13
  136.9 0.4 copy.14
  137.2 0.2 maximum_bitcast_fusion
  137.4 1.6 %copy.16 = bf16[1,2,384,1024]{3,2,1,0:T(8,128)(2,1)} copy(bf16[1,2,384,1024]{2,3,1,0:T(8,128)(2,1)S(1)} %maximum_bitcast_fusion) | data formatting | bytes 3145728
  139.1 2.8 %bitcast_convert_fusion.1 = bf16[4,256,384]{2,1,0:T(8,128)(2,1)} fusion(bf16[4,96,384,1]{2,1,0,3:T(8,128)(2,1)} %bitcast.27, bf16[4,4,96,768]{3,2,1,0:T(8,128)(2,1)} %get-tuple-element.72), kind=kOutput, calls=%fused_computation.39 | convolution fusion | flops 302383104 | bytes 1867776 | tf_op jit(solution)/shard_map/xqrf,xrd->qfd/dot_general | solution.py:280
  141.8 10.0 %all-to-all-done.13 = bf16[32,8,1152]{2,1,0:T(8,128)(2,1)} async-done(((bf16[32,8,1152]{2,1,0:T(8,128)(2,1)}), bf16[32,8,1152]{2,1,0:T(8,128)(2,1)}, u32[]{:S(2)}, u32[]{:S(2)}) %all-to-all-start.13) | async-done | bytes 589856 | tf_op jit(solution)/shard_map/all_to_all | solution.py:262
  151.8 2.3 %shard_map.94 = (bf16[192,384]{1,0:T(8,128)(2,1)}, bf16[192,384]{1,0:T(8,128)(2,1)}) custom-call(s32[1,192]{1,0:T(1,128)} %bitcast.63, f32[1,192]{1,0:T(1,128)} %bitcast.65, bf16[256,1152]{1,0:T(8,128)(2,1)} %bitcast.18.back_ref), custom_call_target="tpu_custom_call" | custom-call | tf_op jit(solution)/shard_map/pallas_call | solution.py:25
  (3 shorter events, 0.1 us)
Async XLA Ops:
  0.6 33.4 %copy-start = (bf16[1,2,384,1024]{3,2,1,0:T(8,128)(2,1)S(1)}, bf16[1,2,384,1024]{3,2,1,0:T(8,128)(2,1)}, u32[]{:S(2)}) copy-start(bf16[1,2,384,1024]{3,2,1,0:T(8,128)(2,1)} %param.14) | copy-start | bytes 4718596
  85.0 13.8 %copy-start.1 = (bf16[1024,384]{1,0:T(8,128)(2,1)S(1)}, bf16[1024,384]{1,0:T(8,128)(2,1)}, u32[]{:S(2)}) copy-start(bf16[1024,384]{1,0:T(8,128)(2,1)} %get-tuple-element.26.w_down_ref) | copy-start | bytes 2359300 | tf_op jit(solution)/shard_map/cond
  103.1 48.7 %all-to-all-start.13 = ((bf16[32,8,1152]{2,1,0:T(8,128)(2,1)}), bf16[32,8,1152]{2,1,0:T(8,128)(2,1)}, u32[]{:S(2)}, u32[]{:S(2)}) async-start(bf16[32,8,1152]{2,1,0:T(8,128)(2,1)} %bitcast.17), calls=%async_computation.13 | async-start | bytes 1179648 | tf_op jit(solution)/shard_map/all_to_all | solution.py:262

commit v5 on v4

--- a/solution.py
+++ b/solution.py
@@ -1,5 +1,6 @@
 import jax
 import jax.numpy as jnp
+import numpy as np
 from jax import lax
 from jax.experimental import pallas as pl
 from jax.experimental.pallas import tpu as pltpu
@@ -9,7 +10,8 @@
 NZ = 4
 EXPERTS = 32
 TOKEN_AXES = ("zl", "y", "core")
-VMEM_BYTES = 56 * 1024 * 1024
+SMALL_GRANT = 20 * 1024 * 1024
+LARGE_GRANT = 56 * 1024 * 1024
 
 
 def dot(a, b, dims):
@@ -20,14 +22,14 @@
     return a.astype(jnp.bfloat16)
 
 
-def kernel_call(body, outs, *args):
+def kernel_call(body, outs, *args, grant=SMALL_GRANT):
     whole = pl.BlockSpec(memory_space=pltpu.VMEM)
     return pl.pallas_call(
         body,
         out_shape=[jax.ShapeDtypeStruct(shape, dtype) for shape, dtype in outs],
         in_specs=[whole] * len(args),
         out_specs=[whole] * len(outs),
-        compiler_params=pltpu.CompilerParams(vmem_limit_bytes=VMEM_BYTES),
+        compiler_params=pltpu.CompilerParams(vmem_limit_bytes=grant),
     )(*args)
 
 
@@ -45,7 +47,8 @@
     return lax.broadcasted_iota(jnp.int32, shape, dim)
 
 
-COUNT_LANES = 128
+MOST = 9
+COUNT_ROW = 3
 MAIN = 8
 REST = 4
 BLOCK_ROWS = EXPERTS * MAIN
@@ -69,10 +72,11 @@
     send_ref[:, feat : 2 * feat] = half(dot(pick, scaled, ((1,), (0,))))
     named = jnp.where(jnp.right_shift(rows, 3) == expert_ref[...], 1.0, 0.0)
     counts = jnp.sum(named, axis=1, keepdims=True)
-    send_ref[:, 3 * feat :] = half(jnp.broadcast_to(counts, (BLOCK_ROWS, COUNT_LANES)))
-    send_ref[:, 2 * feat : 3 * feat] = half(
+    note = (jnp.bitwise_and(iota((BLOCK_ROWS, 1), 0), MAIN - 1) == COUNT_ROW) & (counts <= MOST)
+    send_ref[:, 2 * feat :] = half(
         dot(where_one(rows == rest), tokens, ((1,), (0,)))
         + dot(where_one(rows == rest + REST), scaled, ((1,), (0,)))
+        + jnp.where(note, counts, 0.0)
     )
 
 
@@ -99,17 +103,26 @@
     grad_ref[...] = half(grad)
 
 
-def row_targets(counts):
+def count_sums():
+    i = np.arange(BLOCK_ROWS)[:, None]
+    j = np.arange(BLOCK_ROWS)[None, :]
+    noted = i % MAIN == COUNT_ROW
+    same = noted & (i // MAIN == j // MAIN)
+    earlier = noted & (i // MAIN < j // MAIN)
+    return jnp.asarray(np.concatenate([same, earlier], axis=1), jnp.bfloat16)
+
+
+def row_targets(notes, sums):
     n = BLOCK_ROWS
-    above = iota((n, n), 0)
-    across = iota((n, n), 1)
-    count = jnp.sum(jnp.where(above == across, counts, 0.0), axis=0, keepdims=True)
-    earlier = jnp.right_shift(above, 3) < jnp.right_shift(across, 3)
-    heads = (jnp.bitwise_and(above, MAIN - 1) == 0) & earlier
-    offset = jnp.sum(jnp.where(heads, counts, 0.0), axis=0, keepdims=True)
-    count = count.astype(jnp.int32)
-    offset = offset.astype(jnp.int32)
-    lane = jnp.bitwise_and(iota((1, n), 1), MAIN - 1)
+    lane = iota((1, n), 1)
+    if sums is None:
+        count = jnp.full((1, n), MAIN + REST, jnp.int32)
+        offset = jnp.right_shift(lane, 3) * (MAIN + REST)
+    else:
+        both = dot(notes, sums, ((0,), (0,)))[0:1].astype(jnp.int32)
+        count = both[:, :n]
+        offset = both[:, n:]
+    lane = jnp.bitwise_and(lane, MAIN - 1)
     tail = MAIN + jnp.bitwise_and(lane, REST - 1)
     held = tail < count
     return (
@@ -119,14 +132,17 @@
     )
 
 
-def partial_body(recv_ref, w_gu_ref, w_down_ref, x_ref, s_ref, target_ref, partial_ref):
+def partial_body(recv_ref, w_gu_ref, w_down_ref, *refs):
+    *sums_ref, x_ref, s_ref, target_ref, partial_ref = refs
     part = partial_ref.shape[2]
     rows = NX * part
     room = x_ref.shape[0] // NX
     feat = x_ref.shape[1]
     quarter = w_down_ref.shape[0] // NZ
     index = iota((rows, BLOCK_ROWS), 0)
-    targets = row_targets(recv_ref[:, 3 * feat : 3 * feat + 1].astype(jnp.float32))
+    targets = row_targets(
+        recv_ref[:, 2 * feat : 2 * feat + 128], sums_ref[0][...] if sums_ref else None
+    )
     for k in range(3):
         target_ref[k : k + 1, :] = targets[k]
     pick = where_one(index == targets[0])
@@ -214,7 +230,7 @@
             ((3, BLOCK_ROWS), jnp.int32),
             ((NX, NZ, part, 3 * quarter), bf),
         ],
-        recv, w_gu, w_down,
+        recv, w_gu, w_down, *([] if rows == full_rows else [count_sums()]),
     )
     first = half(add_up(lax.all_to_all(partial, "x", 0, 0, tiled=True)))
     total = add_up(lax.all_to_all(first, "zh", 0, 0, tiled=True))
@@ -255,7 +271,10 @@
     weight_row = router_weight.reshape(1, tok)
     bf = jnp.bfloat16
     (send,) = kernel_call(
-        send_body, [((BLOCK_ROWS, 3 * feat + COUNT_LANES), bf)], expert_row, weight_row, tokens, cotangent
+        send_body,
+        [((BLOCK_ROWS, 3 * feat), bf)],
+        expert_row, weight_row, tokens, cotangent,
+        grant=LARGE_GRANT,
     )
 
     def exchange(values):
@@ -264,8 +283,12 @@
         ).reshape(values.shape)
 
     recv = exchange(send)
-    count = jnp.sum(recv[:, 3 * feat :].astype(jnp.float32)) / (MAIN * COUNT_LANES)
-    level = sum((count > limit).astype(jnp.int32) for limit in LEVELS[:-1])
+    mine = lax.axis_index(TOKEN_AXES).astype(jnp.int32)
+    busy = jnp.sum((expert_of == mine).astype(jnp.int32)) > MOST
+    notes = recv.reshape(EXPERTS, MAIN, 3 * feat)[:, COUNT_ROW, 2 * feat : 2 * feat + 128]
+    count = jnp.sum(notes.astype(jnp.float32)) / 128
+    level = sum((count > limit).astype(jnp.int32) for limit in LEVELS[:-2])
+    level = jnp.where(busy, len(LEVELS) - 1, level)
     back, x_rows, s_rows, full = lax.switch(
         level,
         [lambda *a, n=n: expert_rows(*a, n) for n in LEVELS],

time: 155 us -> 149 us (0.961)
  blocking collectives: 90.7 us -> 61.1 us
  waiting for transfers between devices: 9.99 us -> 24.5 us
  starting transfers between devices: 30.9 us -> 38.6 us
  Pallas kernels: 12.4 us -> 8.95 us
  other arithmetic: 1.03 us -> 2.8 us
  local copies, waits for them, and re-layouts: 2.53 us -> 4.28 us
    all_to_all x1 -> x0, blocking collectives: 29.5 us -> none  [exchange(): lax.all_to_all(values.reshape(EXPERTS, MAIN, values.shape[1]), TOKEN_AXES...]
    all_to_all x1 -> x2, waiting for transfers between devices: 9.99 us -> 24.5 us  [exchange(): lax.all_to_all(values.reshape(EXPERTS, MAIN, values.shape[1]), TOKEN_AXES...]
    all_to_all x1 -> x2, starting transfers between devices: 30.9 us -> 38.6 us  [exchange(): lax.all_to_all(values.reshape(EXPERTS, MAIN, values.shape[1]), TOKEN_AXES...]
    pallas_call x4, Pallas kernels: 12.4 us -> 8.95 us  [kernel_call(): pl.pallas_call(body, out_shape=[jax.ShapeDtypeStruct(shape, dtype) for sh...]
  transfers between devices with their start and end apart: 1 -> 2, of which waited for: 1 -> 2; matrix products, arithmetic and copies ran while one was open for 5% -> 7% of each run, Pallas kernels for 0% -> 0%
where the time goes in v5:
time: 149 us; the launch traced here: 148 us
  blocking collectives  61.1 us (41%)
  starting transfers between devices  38.6 us (26%)
  waiting for transfers between devices  24.5 us (16%)
  Pallas kernels  8.95 us (6%)
  matrix products  5.13 us (3%)
  local copies, waits for them, and re-layouts  4.28 us (3%)
  other arithmetic  2.8 us (2%)
  between operations  2.03 us (1%)
    all_to_all x2, starting transfers between devices, exchange(): lax.all_to_all(values.reshape(EXPERTS, MAIN, values.shape[1]), TOKEN_AXES...  38.6 us
    all_to_all x2, waiting for transfers between devices, exchange(): lax.all_to_all(values.reshape(EXPERTS, MAIN, values.shape[1]), TOKEN_AXES...  24.5 us
    all_to_all x1, blocking collectives, expert_rows(): total = add_up(lax.all_to_all(first, 'zh', 0, 0, tiled=True))  18.7 us
    all_to_all x1, blocking collectives, expert_rows(): first = half(add_up(lax.all_to_all(partial, 'x', 0, 0, tiled=True)))  18.1 us
    all_to_all x1, blocking collectives, expert_rows(): full = lax.all_to_all(copies, 'x', 0, 0, tiled=True)  13 us
    all_gather x1, blocking collectives, expert_rows(): wide = lax.all_gather(piece, 'zh', axis=0, tiled=True)  11.4 us
    pallas_call x4, Pallas kernels, kernel_call(): pl.pallas_call(body, out_shape=[jax.ShapeDtypeStruct(shape, dtype) for sh...  8.95 us
  transfers between devices with their start and end apart: 2, of which 2 were waited for; matrix products, arithmetic and copies ran while one was open for 7% of the time, Pallas kernels for 0%

profile of v5, /device:TPU:1, one launch (start us, length us, event | category | flops | bytes accessed | tf_op | source)
XLA Modules:
  0.0 147.5 jit_solution(5780673882231622860)
XLA Ops:
  0.6 0.0 copy-start.3
  0.6 0.0 copy-start.5
  0.7 2.5 %shard_map.123 = bf16[256,1152]{1,0:T(8,128)(2,1)} custom-call(s32[1,192]{1,0:T(1,128)} %bitcast.47, f32[1,192]{1,0:T(1,128)} %bitcast.49, bf16[192,384]{1,0:T(8,128)(2,1)} %tokens_ref.1, bf16[192,384]{1,0:T(8,128)(2,1)} %cotangent_ref.1), custom_call_target="tpu_custom_call" | custom-call | tf_op jit(solution)/shard_map/pallas_call | solution.py:27
  3.1 10.6 %all-to-all-start.12 = ((bf16[32,8,1152]{2,1,0:T(8,128)(2,1)}), bf16[32,8,1152]{2,1,0:T(8,128)(2,1)S(1)}, u32[]{:S(2)}, u32[]{:S(2)}) async-start(bf16[32,8,1152]{2,1,0:T(8,128)(2,1)} %bitcast.61), calls=%async_computation.12 | async-start | bytes 1179648 | tf_op jit(solution)/shard_map/all_to_all | solution.py:281
  13.7 0.0 copy-done.3
  13.7 0.6 fusion.11
  15.0 16.5 %all-to-all-done.12 = bf16[32,8,1152]{2,1,0:T(8,128)(2,1)S(1)} async-done(((bf16[32,8,1152]{2,1,0:T(8,128)(2,1)}), bf16[32,8,1152]{2,1,0:T(8,128)(2,1)S(1)}, u32[]{:S(2)}, u32[]{:S(2)}) %all-to-all-start.12) | async-done | bytes 589856 | tf_op jit(solution)/shard_map/all_to_all | solution.py:281
  31.5 0.6 fusion.10
  32.8 0.0 copy-done.5
  32.8 67.6 %conditional.1 = (bf16[256,1152]{1,0:T(8,128)(2,1)}, bf16[384,384]{1,0:T(8,128)(2,1)S(1)}, bf16[384,384]{1,0:T(8,128)(2,1)S(1)}, bf16[4,4,96,768]{3,2,1,0:T(8,128)(2,1)}) conditional(s32[]{:T(128)} %clamp.3, (bf16[256,1152]{1,0:T(8,128)(2,1)S(1)}, bf16[1,2,384,1024]{3,2,1,0:T(8,128)(2,1)S(1)}, ...), branch_computations={%region_2.3_spmd, %region_3.4_spmd, %region_4.5_spmd, %region_5.6_... | conditional | flops 3686400 | bytes 22020156 | solution.py:292
  32.8 0.0 copy-start.2
  32.8 0.9 copy-done.2
  33.8 2.4 %branch_0_fun.2 = (bf16[384,384]{1,0:T(8,128)(2,1)S(1)}, bf16[384,384]{1,0:T(8,128)(2,1)S(1)}, s32[3,256]{1,0:T(4,128)S(1)}, bf16[4,4,48,768]{3,2,1,0:T(8,128)(2,1)S(1)}) custom-call(bf16[256,1152]{1,0:T(8,128)(2,1)S(1)} %get-tuple-element.30.recv_ref, bf16[1,2,384,1024]{3,2,1,0:T(8,128)(2,1)S(1)} %get-tuple-element.31.w_gu_ref, ...), custom_call_target="tpu_custom_call" | custom-call | tf_op jit(solution)/shard_map/cond/branch_0_fun/pallas_call | solution.py:27
  36.2 18.1 %all_to_all.58 = bf16[4,4,48,768]{3,2,1,0:T(8,128)(2,1)S(1)} all-to-all(bf16[4,4,48,768]{3,2,1,0:T(8,128)(2,1)S(1)} %get-tuple-element.34), channel_id=1, replica_groups=mesh['zh'=4,'x'=4,'zl'=2,'y'=8,'core'=2] {'x'}, dimensions={0} | all-to-all | bytes 2359296 | tf_op jit(solution)/shard_map/cond/branch_0_fun/all_to_all | solution.py:235
  54.2 0.1 fusion
  54.4 18.7 %all_to_all.59 = bf16[4,48,768]{2,1,0:T(8,128)(2,1)S(1)} all-to-all(bf16[4,48,768]{2,1,0:T(8,128)(2,1)S(1)} %fusion), channel_id=1, replica_groups=mesh['zh'=4,'x'=4,'zl'=2,'y'=8,'core'=2] {'zh'}, dimensions={0} | all-to-all | bytes 589824 | tf_op jit(solution)/shard_map/cond/branch_0_fun/all_to_all | solution.py:236
  73.1 11.4 %all_gather.8 = bf16[192,768]{1,0:T(8,128)(2,1)S(1)} all-gather(bf16[48,768]{1,0:T(8,128)(2,1)S(1)} %pad_maximum_fusion), channel_id=1, replica_groups=mesh['zh'=4,'x'=4,'zl'=2,'y'=8,'core'=2] {'zh'}, dimensions={0}, use_global_device_ids=true | all-gather | bytes 368640 | tf_op jit(solution)/shard_map/cond/branch_0_fun/all_gather | solution.py:252
  84.5 0.1 broadcast_in_dim.19
  84.6 13.0 %all_to_all.60.full_ref = bf16[4,4,48,768]{3,2,1,0:T(8,128)(2,1)S(1)} all-to-all(bf16[4,4,48,768]{3,2,1,0:T(8,128)(2,1)S(1)} %broadcast_in_dim.19), channel_id=1, replica_groups=mesh['zh'=4,'x'=4,'zl'=2,'y'=8,'core'=2] {'x'}, dimensions={0} | all-to-all | bytes 2359296 | tf_op jit(solution)/shard_map/cond/branch_0_fun/all_to_all | solution.py:256
  97.6 0.0 copy-done.6
  97.6 2.8 %branch_0_fun.3 = (bf16[256,1152]{1,0:T(8,128)(2,1)}, bf16[4,4,96,768]{3,2,1,0:T(8,128)(2,1)}) custom-call(bf16[4,4,48,768]{3,2,1,0:T(8,128)(2,1)S(1)} %all_to_all.60.full_ref, s32[3,256]{1,0:T(4,128)S(1)} %get-tuple-element.35.target_ref, bf16[1,2,384,1024]{3,2,1,0:T(8,128)(2,1)S(1)} %get-tuple-element.31.w_gu_ref, bf16[1024,384]{1,0:T(8,128)(2,1)S(1)} %copy-done.6), custom_call_target="tpu_custom_call" | custom-call | tf_op jit(solution)/shard_map/cond/branch_0_fun/pallas_call | solution.py:27
  100.4 28.1 %all-to-all-start.13 = ((bf16[32,8,1152]{2,1,0:T(8,128)(2,1)}), bf16[32,8,1152]{2,1,0:T(8,128)(2,1)S(1)}, u32[]{:S(2)}, u32[]{:S(2)}) async-start(bf16[32,8,1152]{2,1,0:T(8,128)(2,1)} %bitcast.17), calls=%async_computation.13 | async-start | bytes 1179648 | tf_op jit(solution)/shard_map/all_to_all | solution.py:281
  128.5 2.4 %bitcast_convert_fusion = bf16[384,4,512]{2,0,1:T(8,128)(2,1)S(1)} fusion(bf16[4,96,384,1]{2,1,0,3:T(8,128)(2,1)S(1)} %bitcast.66, bf16[4,4,96,768]{3,2,1,0:T(8,128)(2,1)} %get-tuple-element.81), kind=kOutput, calls=%fused_computation.36 | convolution fusion | flops 604766208 | bytes 3440640 | tf_op jit(solution)/shard_map/xrd,xqrf->dqf/dot_general | solution.py:300
  130.9 0.1 fusion.12
  131.0 0.4 copy.19
  131.4 1.2 copy.20
  132.6 1.3 maximum_bitcast_fusion
  133.9 1.6 %copy.22 = bf16[1,2,384,1024]{3,2,1,0:T(8,128)(2,1)} copy(bf16[1,2,384,1024]{2,3,1,0:T(8,128)(2,1)S(1)} %maximum_bitcast_fusion) | data formatting | bytes 3145728
  135.5 2.7 %bitcast_convert_fusion.1 = bf16[4,256,384]{2,1,0:T(8,128)(2,1)} fusion(bf16[4,96,384,1]{2,1,0,3:T(8,128)(2,1)S(1)} %bitcast.67, bf16[4,4,96,768]{3,2,1,0:T(8,128)(2,1)} %get-tuple-element.81), kind=kOutput, calls=%fused_computation.39 | convolution fusion | flops 302383104 | bytes 1867776 | tf_op jit(solution)/shard_map/xqrf,xrd->qfd/dot_general | solution.py:303
  138.2 8.1 %all-to-all-done.13 = bf16[32,8,1152]{2,1,0:T(8,128)(2,1)S(1)} async-done(((bf16[32,8,1152]{2,1,0:T(8,128)(2,1)}), bf16[32,8,1152]{2,1,0:T(8,128)(2,1)S(1)}, u32[]{:S(2)}, u32[]{:S(2)}) %all-to-all-start.13) | async-done | bytes 589856 | tf_op jit(solution)/shard_map/all_to_all | solution.py:281
  146.3 0.0 copy-done.4
  146.3 1.2 shard_map.124
  (5 shorter events, 0.1 us)
Async XLA Ops:
  0.6 13.1 %copy-start.3 = (s32[192]{0:T(256)S(1)}, s32[192]{0:T(256)}, u32[]{:S(2)}) copy-start(s32[192]{0:T(256)} %param.14) | copy-start | bytes 2308
  0.6 32.1 %copy-start.5 = (bf16[1,2,384,1024]{3,2,1,0:T(8,128)(2,1)S(1)}, bf16[1,2,384,1024]{3,2,1,0:T(8,128)(2,1)}, u32[]{:S(2)}) copy-start(bf16[1,2,384,1024]{3,2,1,0:T(8,128)(2,1)} %param.17) | copy-start | bytes 4718596
  3.1 28.3 %all-to-all-start.12 = ((bf16[32,8,1152]{2,1,0:T(8,128)(2,1)}), bf16[32,8,1152]{2,1,0:T(8,128)(2,1)S(1)}, u32[]{:S(2)}, u32[]{:S(2)}) async-start(bf16[32,8,1152]{2,1,0:T(8,128)(2,1)} %bitcast.61), calls=%async_computation.12 | async-start | bytes 1179648 | tf_op jit(solution)/shard_map/all_to_all | solution.py:281
  32.8 1.0 copy-start.2
  84.5 13.1 %copy-start.6 = (bf16[1024,384]{1,0:T(8,128)(2,1)S(1)}, bf16[1024,384]{1,0:T(8,128)(2,1)}, u32[]{:S(2)}) copy-start(bf16[1024,384]{1,0:T(8,128)(2,1)} %get-tuple-element.32.w_down_ref) | copy-start | bytes 2359300 | tf_op jit(solution)/shard_map/cond
  100.4 45.9 %all-to-all-start.13 = ((bf16[32,8,1152]{2,1,0:T(8,128)(2,1)}), bf16[32,8,1152]{2,1,0:T(8,128)(2,1)S(1)}, u32[]{:S(2)}, u32[]{:S(2)}) async-start(bf16[32,8,1152]{2,1,0:T(8,128)(2,1)} %bitcast.17), calls=%async_computation.13 | async-start | bytes 1179648 | tf_op jit(solution)/shard_map/all_to_all | solution.py:281
  135.5 10.8 %copy-start.4 = (f32[192]{0:T(256)S(1)}, f32[192]{0:T(256)}, u32[]{:S(2)}) copy-start(f32[192]{0:T(256)} %param.15) | copy-start | bytes 2308

commit v6 on v5

--- a/solution.py
+++ b/solution.py
@@ -285,13 +285,21 @@
     recv = exchange(send)
     mine = lax.axis_index(TOKEN_AXES).astype(jnp.int32)
     busy = jnp.sum((expert_of == mine).astype(jnp.int32)) > MOST
-    notes = recv.reshape(EXPERTS, MAIN, 3 * feat)[:, COUNT_ROW, 2 * feat : 2 * feat + 128]
-    count = jnp.sum(notes.astype(jnp.float32)) / 128
-    level = sum((count > limit).astype(jnp.int32) for limit in LEVELS[:-2])
-    level = jnp.where(busy, len(LEVELS) - 1, level)
-    back, x_rows, s_rows, full = lax.switch(
-        level,
-        [lambda *a, n=n: expert_rows(*a, n) for n in LEVELS],
+
+    def other(recv, w_gu, w_down):
+        notes = recv.reshape(EXPERTS, MAIN, 3 * feat)[:, COUNT_ROW, 2 * feat : 2 * feat + 128]
+        count = jnp.sum(notes.astype(jnp.float32)) / 128
+        level = sum((count > limit).astype(jnp.int32) for limit in LEVELS[:-2])
+        return lax.switch(
+            level,
+            [lambda *a, n=n: expert_rows(*a, n) for n in LEVELS[:-1]],
+            recv, w_gu, w_down,
+        )
+
+    back, x_rows, s_rows, full = lax.cond(
+        busy,
+        lambda *a: expert_rows(*a, LEVELS[-1]),
+        other,
         recv, gate_up_weight, w_down,
     )
     back = exchange(back)

time: 149 us -> 152 us (1.020)
  starting transfers between devices: 38.6 us -> 42.3 us
    all_to_all x2, starting transfers between devices: 38.6 us -> 42.3 us  [exchange(): lax.all_to_all(values.reshape(EXPERTS, MAIN, values.shape[1]), TOKEN_AXES...]
where the time goes in v6:
time: 152 us; the launch traced here: 151 us
  blocking collectives  61.4 us (40%)
  starting transfers between devices  42.3 us (28%)
  waiting for transfers between devices  24.5 us (16%)
  Pallas kernels  9 us (6%)
  matrix products  5.13 us (3%)
  local copies, waits for them, and re-layouts  3.33 us (2%)
  other arithmetic  2.8 us (2%)
    all_to_all x2, starting transfers between devices, exchange(): lax.all_to_all(values.reshape(EXPERTS, MAIN, values.shape[1]), TOKEN_AXES...  42.3 us
    all_to_all x2, waiting for transfers between devices, exchange(): lax.all_to_all(values.reshape(EXPERTS, MAIN, values.shape[1]), TOKEN_AXES...  24.5 us
    all_to_all x1, blocking collectives, expert_rows(): first = half(add_up(lax.all_to_all(partial, 'x', 0, 0, tiled=True)))  18.1 us
    all_to_all x1, blocking collectives, expert_rows(): total = add_up(lax.all_to_all(first, 'zh', 0, 0, tiled=True))  17.7 us
    all_to_all x1, blocking collectives, expert_rows(): full = lax.all_to_all(copies, 'x', 0, 0, tiled=True)  13 us
    all_gather x1, blocking collectives, expert_rows(): wide = lax.all_gather(piece, 'zh', axis=0, tiled=True)  12.6 us
    pallas_call x4, Pallas kernels, kernel_call(): pl.pallas_call(body, out_shape=[jax.ShapeDtypeStruct(shape, dtype) for sh...  9 us
  transfers between devices with their start and end apart: 2, of which 2 were waited for; matrix products, arithmetic and copies ran while one was open for 7% of the time, Pallas kernels for 0%

profile of v6, /device:TPU:1, one launch (start us, length us, event | category | flops | bytes accessed | tf_op | source)
XLA Modules:
  0.0 150.5 jit_solution(3378619446668725484)
XLA Ops:
  0.6 0.0 copy-start
  0.6 0.0 copy-start.2
  0.7 2.5 %shard_map.121 = bf16[256,1152]{1,0:T(8,128)(2,1)} custom-call(s32[1,192]{1,0:T(1,128)} %bitcast.47, f32[1,192]{1,0:T(1,128)} %bitcast.49, bf16[192,384]{1,0:T(8,128)(2,1)} %tokens_ref.1, bf16[192,384]{1,0:T(8,128)(2,1)} %cotangent_ref.1), custom_call_target="tpu_custom_call" | custom-call | tf_op jit(solution)/shard_map/pallas_call | solution.py:27
  3.1 10.6 %all-to-all-start.12 = ((bf16[32,8,1152]{2,1,0:T(8,128)(2,1)}), bf16[32,8,1152]{2,1,0:T(8,128)(2,1)S(1)}, u32[]{:S(2)}, u32[]{:S(2)}) async-start(bf16[32,8,1152]{2,1,0:T(8,128)(2,1)} %bitcast.58), calls=%async_computation.12 | async-start | bytes 1179648 | tf_op jit(solution)/shard_map/all_to_all | solution.py:281
  13.7 0.0 copy-done
  13.7 0.6 fusion.10
  15.0 16.5 %all-to-all-done.12 = bf16[32,8,1152]{2,1,0:T(8,128)(2,1)S(1)} async-done(((bf16[32,8,1152]{2,1,0:T(8,128)(2,1)}), bf16[32,8,1152]{2,1,0:T(8,128)(2,1)S(1)}, u32[]{:S(2)}, u32[]{:S(2)}) %all-to-all-start.12) | async-done | bytes 589856 | tf_op jit(solution)/shard_map/all_to_all | solution.py:281
  31.5 0.0 copy-done.2
  31.5 68.3 %conditional.2 = (bf16[256,1152]{1,0:T(8,128)(2,1)}, bf16[4,4,96,768]{3,2,1,0:T(8,128)(2,1)}, bf16[384,384]{1,0:T(8,128)(2,1)S(1)}, bf16[384,384]{1,0:T(8,128)(2,1)S(1)}) conditional(s32[]{:T(128)} %convert_element_type.178, (bf16[32,8,1152]{2,1,0:T(8,128)(2,1)S(1)}, bf16[256,1152]{1,0:T(8,128)(2,1)S(1)}, bf16[1,2,384,1024]{3,2,1,0:T(8,128)(2,1)S(1)}, ...), branch_computations={%region_1.0_spmd, %region_6.0_spmd} | conditional | flops 3686400 | bytes 22020156 | solution.py:299
  31.5 0.6 convert_reduce_fusion
  32.8 67.0 %conditional = (bf16[256,1152]{1,0:T(8,128)(2,1)}, bf16[384,384]{1,0:T(8,128)(2,1)S(1)}, bf16[384,384]{1,0:T(8,128)(2,1)S(1)}, bf16[4,4,96,768]{3,2,1,0:T(8,128)(2,1)}) conditional(s32[]{:T(128)} %clamp.2, (bf16[256,1152]{1,0:T(8,128)(2,1)S(1)}, bf16[1,2,384,1024]{3,2,1,0:T(8,128)(2,1)S(1)}, bf16[1024,384]{1,0:T(8,128)(2,1)}, ...), branch_computations={%region_3.0_spmd, %region_4.0_spmd, %region_5.0_spmd} | conditional | flops 2764800 | bytes 17301564 | solution.py:293
  32.8 2.4 %branch_0_fun.2 = (bf16[384,384]{1,0:T(8,128)(2,1)S(1)}, bf16[384,384]{1,0:T(8,128)(2,1)S(1)}, s32[3,256]{1,0:T(4,128)S(1)}, bf16[4,4,48,768]{3,2,1,0:T(8,128)(2,1)S(1)}) custom-call(bf16[256,1152]{1,0:T(8,128)(2,1)S(1)} %get-tuple-element.54.recv_ref, bf16[1,2,384,1024]{3,2,1,0:T(8,128)(2,1)S(1)} %get-tuple-element.55.w_gu_ref, ...), custom_call_target="tpu_custom_call" | custom-call | tf_op jit(solution)/shard_map/cond/branch_0_fun/cond/branch_0_fun/pallas_call | solution.py:27
  35.2 18.1 %all_to_all.58 = bf16[4,4,48,768]{3,2,1,0:T(8,128)(2,1)S(1)} all-to-all(bf16[4,4,48,768]{3,2,1,0:T(8,128)(2,1)S(1)} %get-tuple-element.58), channel_id=1, replica_groups=mesh['zh'=4,'x'=4,'zl'=2,'y'=8,'core'=2] {'x'}, dimensions={0} | all-to-all | bytes 2359296 | tf_op jit(solution)/shard_map/cond/branch_0_fun/cond/branch_0_fun/all_to_all | solution.py:235
  53.3 0.1 fusion
  53.4 17.7 %all_to_all.59 = bf16[4,48,768]{2,1,0:T(8,128)(2,1)S(1)} all-to-all(bf16[4,48,768]{2,1,0:T(8,128)(2,1)S(1)} %fusion), channel_id=1, replica_groups=mesh['zh'=4,'x'=4,'zl'=2,'y'=8,'core'=2] {'zh'}, dimensions={0} | all-to-all | bytes 589824 | tf_op jit(solution)/shard_map/cond/branch_0_fun/cond/branch_0_fun/all_to_all | solution.py:236
  71.3 12.6 %all_gather.8 = bf16[192,768]{1,0:T(8,128)(2,1)S(1)} all-gather(bf16[48,768]{1,0:T(8,128)(2,1)S(1)} %pad_maximum_fusion), channel_id=1, replica_groups=mesh['zh'=4,'x'=4,'zl'=2,'y'=8,'core'=2] {'zh'}, dimensions={0}, use_global_device_ids=true | all-gather | bytes 368640 | tf_op jit(solution)/shard_map/cond/branch_0_fun/cond/branch_0_fun/all_gather | solution.py:252
  83.8 0.0 copy-start.3
  83.8 0.1 broadcast_in_dim.19
  83.9 13.0 %all_to_all.60.full_ref = bf16[4,4,48,768]{3,2,1,0:T(8,128)(2,1)S(1)} all-to-all(bf16[4,4,48,768]{3,2,1,0:T(8,128)(2,1)S(1)} %broadcast_in_dim.19), channel_id=1, replica_groups=mesh['zh'=4,'x'=4,'zl'=2,'y'=8,'core'=2] {'x'}, dimensions={0} | all-to-all | bytes 2359296 | tf_op jit(solution)/shard_map/cond/branch_0_fun/cond/branch_0_fun/all_to_all | solution.py:256
  96.9 0.0 copy-done.3
  96.9 2.8 %branch_0_fun.3 = (bf16[256,1152]{1,0:T(8,128)(2,1)}, bf16[4,4,96,768]{3,2,1,0:T(8,128)(2,1)}) custom-call(bf16[4,4,48,768]{3,2,1,0:T(8,128)(2,1)S(1)} %all_to_all.60.full_ref, s32[3,256]{1,0:T(4,128)S(1)} %get-tuple-element.59.target_ref, bf16[1,2,384,1024]{3,2,1,0:T(8,128)(2,1)S(1)} %get-tuple-element.55.w_gu_ref, bf16[1024,384]{1,0:T(8,128)(2,1)S(1)} %copy-done.3), custom_call_target="tpu_custom_call" | custom-call | tf_op jit(solution)/shard_map/cond/branch_0_fun/cond/branch_0_fun/pallas_call | solution.py:27
  99.8 31.7 %all-to-all-start.13 = ((bf16[32,8,1152]{2,1,0:T(8,128)(2,1)}), bf16[32,8,1152]{2,1,0:T(8,128)(2,1)S(1)}, u32[]{:S(2)}, u32[]{:S(2)}) async-start(bf16[32,8,1152]{2,1,0:T(8,128)(2,1)} %bitcast.17), calls=%async_computation.13 | async-start | bytes 1179648 | tf_op jit(solution)/shard_map/all_to_all | solution.py:281
  131.5 2.4 %bitcast_convert_fusion = bf16[384,4,512]{2,0,1:T(8,128)(2,1)S(1)} fusion(bf16[4,96,384,1]{2,1,0,3:T(8,128)(2,1)S(1)} %bitcast.63, bf16[4,4,96,768]{3,2,1,0:T(8,128)(2,1)} %get-tuple-element.116), kind=kOutput, calls=%fused_computation.37 | convolution fusion | flops 604766208 | bytes 3440640 | tf_op jit(solution)/shard_map/xrd,xqrf->dqf/dot_general | solution.py:308
  133.9 0.1 fusion.11
  134.1 0.4 copy.17
  134.4 1.2 copy.18
  135.6 1.3 maximum_bitcast_fusion
  136.9 1.6 %copy.20 = bf16[1,2,384,1024]{3,2,1,0:T(8,128)(2,1)} copy(bf16[1,2,384,1024]{2,3,1,0:T(8,128)(2,1)S(1)} %maximum_bitcast_fusion) | data formatting | bytes 3145728
  138.5 2.7 %bitcast_convert_fusion.1 = bf16[4,256,384]{2,1,0:T(8,128)(2,1)} fusion(bf16[4,96,384,1]{2,1,0,3:T(8,128)(2,1)S(1)} %bitcast.64, bf16[4,4,96,768]{3,2,1,0:T(8,128)(2,1)} %get-tuple-element.116), kind=kOutput, calls=%fused_computation.40 | convolution fusion | flops 302383104 | bytes 1867776 | tf_op jit(solution)/shard_map/xqrf,xrd->qfd/dot_general | solution.py:311
  141.2 8.1 %all-to-all-done.13 = bf16[32,8,1152]{2,1,0:T(8,128)(2,1)S(1)} async-done(((bf16[32,8,1152]{2,1,0:T(8,128)(2,1)}), bf16[32,8,1152]{2,1,0:T(8,128)(2,1)S(1)}, u32[]{:S(2)}, u32[]{:S(2)}) %all-to-all-start.13) | async-done | bytes 589856 | tf_op jit(solution)/shard_map/all_to_all | solution.py:281
  149.3 0.0 copy-done.1
  149.3 1.2 shard_map.122
  (4 shorter events, 0.1 us)
Async XLA Ops:
  0.6 13.1 %copy-start = (s32[192]{0:T(256)S(1)}, s32[192]{0:T(256)}, u32[]{:S(2)}) copy-start(s32[192]{0:T(256)} %param.15) | copy-start | bytes 2308
  0.6 30.8 %copy-start.2 = (bf16[1,2,384,1024]{3,2,1,0:T(8,128)(2,1)S(1)}, bf16[1,2,384,1024]{3,2,1,0:T(8,128)(2,1)}, u32[]{:S(2)}) copy-start(bf16[1,2,384,1024]{3,2,1,0:T(8,128)(2,1)} %param.18) | copy-start | bytes 4718596
  3.1 28.3 %all-to-all-start.12 = ((bf16[32,8,1152]{2,1,0:T(8,128)(2,1)}), bf16[32,8,1152]{2,1,0:T(8,128)(2,1)S(1)}, u32[]{:S(2)}, u32[]{:S(2)}) async-start(bf16[32,8,1152]{2,1,0:T(8,128)(2,1)} %bitcast.58), calls=%async_computation.12 | async-start | bytes 1179648 | tf_op jit(solution)/shard_map/all_to_all | solution.py:281
  83.8 13.1 %copy-start.3 = (bf16[1024,384]{1,0:T(8,128)(2,1)S(1)}, bf16[1024,384]{1,0:T(8,128)(2,1)}, u32[]{:S(2)}) copy-start(bf16[1024,384]{1,0:T(8,128)(2,1)} %get-tuple-element.56.w_down_ref) | copy-start | bytes 2359300 | tf_op jit(solution)/shard_map/cond/branch_0_fun/cond
  99.8 49.5 %all-to-all-start.13 = ((bf16[32,8,1152]{2,1,0:T(8,128)(2,1)}), bf16[32,8,1152]{2,1,0:T(8,128)(2,1)S(1)}, u32[]{:S(2)}, u32[]{:S(2)}) async-start(bf16[32,8,1152]{2,1,0:T(8,128)(2,1)} %bitcast.17), calls=%async_computation.13 | async-start | bytes 1179648 | tf_op jit(solution)/shard_map/all_to_all | solution.py:281
  138.5 10.8 %copy-start.1 = (f32[192]{0:T(256)S(1)}, f32[192]{0:T(256)}, u32[]{:S(2)}) copy-start(f32[192]{0:T(256)} %param.16) | copy-start | bytes 2308
